TPU v7x, 512 devices: a whole 4x4x16 slice. The times are simulated.
512 devices in a mesh: row: 16 (over z_hi, x), col: 32 (over y, z_lo, core).
Axes of the slice: x: 4, y: 4, z: 16 (z_hi: 4, z_lo: 4; z = z_hi * 4 + z_lo), core: 2. Of those that a mesh axis runs over, the one named last changes fastest.
Arguments:
- features: bfloat16 [64, 2048, 2048], P(None, 'col', 'row'), may hold values from -6 to 6
- conv_weight: bfloat16 [3, 3, 64, 64], replicated, may hold values from -0.25 to 0.25
- conv_bias: float32 [64], replicated, may hold values from -3 to 3
- head_weight: bfloat16 [62, 64], replicated, may hold values from -40 to 40
- head_bias: float32 [62], replicated, may hold values from -4 to 4
- dist_label: int32 [2048, 2048], P('col', 'row'), may hold values from 0 to 36, as said below
- omega_label: int32 [2048, 2048], P('col', 'row'), may hold values from 0 to 24, as said below
- residue_mask: int32 [2048], replicated, may hold values from 0 to 1, as said below
Outputs:
- grad_input: bfloat16 [64, 2048, 2048], P(None, 'col', 'row')
- grad_conv_weight: float32 [3, 3, 64, 64], replicated
- grad_conv_bias: float32 [64], replicated
- grad_head_weight: float32 [62, 64], replicated
- grad_head_bias: float32 [62], replicated
Inputs may be any that keep to these rules, and one draw needn't show every extreme that they name: dist_label[i, j] = dist_label[j, i]. omega_label[i, j] = omega_label[j, i]. `residue_mask`: at least one residue has coordinates.
All inputs are finite; a program needn't handle non-finite values.
Results may differ from a plain program's by a relative error of at most 0.0025.
The roundings to bfloat16 on the way count: a program that leaves them out, or rounds other values in their place, can miss the bound.
Values may be sent and summed in bfloat16 or wider, within the bound.
A program may use at most 64 MiB of HBM per device.

v0:
```python
import jax
import jax.numpy as jnp
from jax import lax
from jax.sharding import PartitionSpec as P

DILATION_STEP = 16
DB = 37


def with_halo(cells, sides, width):
    for axis, dim in sides:
        count = lax.axis_size(axis)
        ends = count - 1
        head = lax.slice_in_dim(cells, 0, width, axis=dim)
        tail = lax.slice_in_dim(cells, cells.shape[dim] - width, cells.shape[dim], axis=dim)
        cells = jnp.concatenate(
            [
                lax.ppermute(tail, axis, [(i, (i + 1) % count) for i in range(ends)]),
                cells,
                lax.ppermute(head, axis, [((i + 1) % count, i) for i in range(ends)]),
            ],
            axis=dim,
        )
    return cells


def extend(receptive_field, which):
    if which == "act":
        return with_halo(receptive_field, (("col", 1), ("row", 2)), DILATION_STEP)
    return with_halo(receptive_field, (("col", 1), ("row", 2)), DILATION_STEP)


def tap_stack(extended_input, first_member, row_span, column_span):
    start = first_member * DILATION_STEP
    band = extended_input[:, start : start + row_span, :]
    pieces = [
        band[:, :, second_member * DILATION_STEP : second_member * DILATION_STEP + column_span]
        for second_member in range(3)
    ]
    return jnp.concatenate(pieces, axis=0)


def tap_matrix(weight, first_member):
    channels_out = weight.shape[2]
    channels_in = weight.shape[3]
    return jnp.transpose(weight[first_member], (1, 0, 2)).reshape(channels_out, 3 * channels_in)


def dilated(extended_input, weight, row_span, column_span):
    total = None
    for first_member in range(3):
        stacked = tap_stack(extended_input, first_member, row_span, column_span)
        term = jnp.einsum(
            "ok,kxy->oxy",
            tap_matrix(weight, first_member),
            stacked,
            preferred_element_type=jnp.float32,
        )
        total = term if total is None else total + term
    return total


def mirror(logits):
    bins, row_span, column_span = logits.shape
    ncol = lax.axis_size("col")
    nrow = lax.axis_size("row")
    ratio = ncol // nrow
    piece = row_span // ncol
    sectioned = logits.reshape(bins, row_span, ratio, ncol, piece)
    moved = lax.all_to_all(
        lax.all_to_all(sectioned, "col", split_axis=3, concat_axis=1, tiled=True),
        "row",
        split_axis=1,
        concat_axis=3,
        tiled=True,
    )
    ordered = jnp.transpose(moved, (0, 3, 2, 1, 4)).reshape(bins, ncol, column_span, piece)
    placed = lax.all_to_all(ordered, "col", split_axis=1, concat_axis=3, tiled=True)
    return jnp.transpose(placed.reshape(bins, column_span, row_span), (0, 2, 1))


def group_grad(scores, labels):
    prob = jax.nn.softmax(scores, axis=0)
    onehot = (jnp.arange(scores.shape[0], dtype=jnp.int32)[:, None, None] == labels[None]).astype(
        jnp.float32
    )
    return prob - onehot


def per_device(
    features, conv_weight, conv_bias, head_weight, head_bias, dist_label, omega_label, residue_mask
):
    channels, row_span, column_span = features.shape
    x32 = features.astype(jnp.float32)
    act = jax.nn.elu(x32).astype(jnp.bfloat16)
    activation_extended = extend(act, "act")
    pre = (
        dilated(activation_extended, conv_weight, row_span, column_span) + conv_bias[:, None, None]
    )
    mixed = (x32 + pre).astype(jnp.bfloat16)
    logits = (
        jnp.einsum("nc,cxy->nxy", head_weight, mixed, preferred_element_type=jnp.float32)
        + head_bias[:, None, None]
    ).astype(jnp.bfloat16)
    mirrored = mirror(logits)
    sym = 0.5 * (logits.astype(jnp.float32) + mirrored.astype(jnp.float32))
    mask = residue_mask.astype(jnp.float32)
    mask_first = lax.dynamic_slice_in_dim(mask, lax.axis_index("col") * row_span, row_span)
    mask_second = lax.dynamic_slice_in_dim(mask, lax.axis_index("row") * column_span, column_span)
    pair = mask_first[:, None] * mask_second[None, :]
    count = jnp.sum(mask)
    grad_sym = (
        jnp.concatenate(
            [group_grad(sym[:DB], dist_label), group_grad(sym[DB:], omega_label)], axis=0
        )
        * pair[None]
    )
    grad_logit = grad_sym.astype(jnp.bfloat16)
    grad_mixed = jnp.einsum(
        "nc,nxy->cxy", head_weight, grad_logit, preferred_element_type=jnp.float32
    )
    head_w_term = jnp.einsum("nxy,cxy->nc", grad_logit, mixed, preferred_element_type=jnp.float32)
    head_b_term = jnp.sum(grad_sym, axis=(1, 2))
    grad_pre = grad_mixed.astype(jnp.bfloat16)
    grad_wide = extend(grad_pre, "grad")
    flipped = jnp.transpose(conv_weight[::-1, ::-1], (0, 1, 3, 2))
    grad_act = dilated(grad_wide, flipped, row_span, column_span)
    tap_rows = []
    for first_member in range(3):
        stacked = tap_stack(activation_extended, first_member, row_span, column_span)
        flat = jnp.einsum("oxy,kxy->ok", grad_pre, stacked, preferred_element_type=jnp.float32)
        tap_rows.append(jnp.transpose(flat.reshape(channels, 3, channels), (1, 0, 2)))
    conv_w_term = jnp.stack(tap_rows, 0)
    conv_b_term = jnp.sum(grad_mixed, axis=(1, 2))
    conv_w_sum, conv_b_sum, head_w_sum, head_b_sum = lax.psum(
        (conv_w_term, conv_b_term, head_w_term, head_b_term), ("row", "col")
    )
    slope = jnp.where(x32 > 0.0, jnp.float32(1.0), jnp.exp(jnp.minimum(x32, 0.0)))
    grad_input = (grad_mixed + slope * grad_act).astype(jnp.bfloat16)
    return (
        grad_input,
        conv_w_sum / count,
        conv_b_sum / count,
        head_w_sum / count,
        head_b_sum / count,
    )


def solution(mesh):
    return jax.shard_map(
        per_device,
        mesh=mesh,
        in_specs=(P(None, "col", "row"), P(), P(), P(), P(), P("col", "row"), P("col", "row"), P()),
        out_specs=(P(None, "col", "row"), P(), P(), P(), P()),
        check_vma=False,
    )
```

profile of v0, /device:TPU:1, one launch (start us, length us, event | category | flops | bytes accessed | tf_op | source)
XLA Modules:
  0.0 905.4 jit_solution(6945523647584539868)
XLA Ops:
  7.2 2.4 fusion.31
  9.6 4.9 collective-permute-start
  14.5 5.2 collective-permute-start.1
  19.7 4.0 collective-permute-done.1
  23.9 1.8 fusion.75
  25.8 3.3 copy.64
  29.1 3.8 collective-permute-start.2
  32.9 2.3 copy.66
  37.0 3.1 copy.65
  40.1 2.5 collective-permute-done.3
  42.6 3.9 copy.67
  46.5 7.9 maximum_maximum_fusion
  54.4 1.8 fusion.71
  59.5 7.4 fusion.32
  67.4 2.5 copy.74
  69.8 4.3 copy.122
  74.1 5.5 reshape.109
  79.6 36.5 %all_to_all.45 = bf16[32,2,7936]{2,1,0:T(2,128)(2,1)} all-to-all(bf16[32,2,7936]{2,1,0:T(2,128)(2,1)} %reshape.109), channel_id=1, replica_groups=mesh['row'=16,'col'=32] {'col'}, dimensions={0} | all-to-all | bytes 2031616 | tf_op jit(solution)/shard_map/all_to_all | solution.py:71
  116.1 5.7 reshape.110
  121.7 4.3 bitcast_bitcast_fusion
  126.0 7.8 copy.108
  133.8 8.6 reshape.111
  142.4 90.6 %all_to_all.46 = bf16[16,2,15872]{2,1,0:T(2,128)(2,1)} all-to-all(bf16[16,2,15872]{2,1,0:T(2,128)(2,1)} %reshape.111), channel_id=1, replica_groups=mesh['row'=16,'col'=32] {'row'}, dimensions={0} | all-to-all | bytes 2031616 | tf_op jit(solution)/shard_map/all_to_all | solution.py:70
  233.0 10.0 %reshape.112 = bf16[2048,1,2,2,62]{4,3,2,1,0:T(2,128)(2,1)} reshape(bf16[16,2,15872]{2,1,0:T(2,128)(2,1)} %all_to_all.46) | data formatting | bytes 2031616
  243.0 4.3 copy.109
  247.4 2.8 copy.79
  250.2 1.7 copy.80
  251.9 6.3 all-to-all-start.2
  260.7 24.9 %all-to-all-done.2 = bf16[62,32,128,2]{2,3,0,1:T(2,128)(2,1)} async-done(((bf16[62,32,128,2]{2,3,0,1:T(2,128)(2,1)}), bf16[62,32,128,2]{2,3,0,1:T(2,128)(2,1)}, u32[]{:S(2)}, u32[]{:S(2)}) %all-to-all-start.2) | async-done | bytes 1015840 | tf_op jit(solution)/shard_map/all_to_all | solution.py:78
  285.6 1.9 convert_bitcast_fusion
  288.3 2.3 fusion.80
  290.6 2.3 fusion.79
  294.4 2.0 fusion.73
  298.9 100.1 %all-reduce = (f32[64]{0:T(128)S(1)}, f32[62,64]{1,0:T(8,128)S(1)}, f32[62]{0:T(128)S(1)}) all-reduce(f32[64]{0:T(128)S(1)} %get-tuple-element.40, f32[62,64]{1,0:T(8,128)S(1)} %convolution_bitcast_fusion, f32[62]{0:T(128)S(1)} %fusion.37), channel_id=1, replica_groups=mesh['row'=16,'col'=32] {'row','col'}, use_global_device_ids=true, to_apply=%region_7.8 | all-reduce | flops 4094 | bytes 32752 | tf_op jit(solution)/shard_map/psum | solution.py:135
  401.2 4.2 collective-permute-start.4
  405.5 2.1 collective-permute-start.5
  407.6 3.1 fusion.46
  415.5 2.3 fusion.74
  417.8 2.6 copy.83
  420.4 2.1 collective-permute-start.6
  422.5 2.7 copy.85
  426.5 449.6 %all-reduce.3.cloned.1.call-done = f32[3,3,64,64]{2,3,1,0:T(8,128)} async-done(((f32[3,3,64,64]{2,3,1,0:T(8,128)}), f32[3,3,64,64]{2,3,1,0:T(8,128)}) %all-reduce.3.cloned.1.call-update) | async-done | bytes 147472 | tf_op jit(solution)/shard_map/psum | solution.py:135
  878.6 3.1 copy.84
  881.6 3.0 copy.86
  884.7 4.9 maximum_maximum_fusion.1
  892.1 1.9 fusion.10
  894.1 2.7 fusion.29
  896.7 1.6 copy.93
  (101 shorter events, 26.2 us)
Async XLA Ops:
  7.2 59.8 %copy-start = (bf16[62,64]{1,0:T(8,128)(2,1)S(1)}, bf16[62,64]{1,0:T(8,128)(2,1)}, u32[]{:S(2)}) copy-start(bf16[62,64]{1,0:T(8,128)(2,1)} %param.11) | copy-start | bytes 23812
  9.6 10.1 %collective-permute-start = (bf16[64,16,128]{2,0,1:T(8,128)(2,1)S(1)}, bf16[64,16,128]{2,0,1:T(8,128)(2,1)S(1)}, u32[]{:S(2)}, u32[]{:S(2)}) collective-permute-start(bf16[64,16,128]{2,0,1:T(8,128)(2,1)S(1)} %get-tuple-element.53), channel_id=1, source_target_pairs={{0,1},{1,2},{2,3},{3,4},{4,5},{5,6},{6,7},{7,8},{8,9},{9,10},{10,1... | collective-permute-start | bytes 786440 | tf_op jit(solution)/shard_map/ppermute | solution.py:18
  14.5 9.2 %collective-permute-start.1 = (bf16[64,16,128]{2,0,1:T(8,128)(2,1)S(1)}, bf16[64,16,128]{2,0,1:T(8,128)(2,1)S(1)}, u32[]{:S(2)}, u32[]{:S(2)}) collective-permute-start(bf16[64,16,128]{2,0,1:T(8,128)(2,1)S(1)} %get-tuple-element.52), channel_id=1, source_target_pairs={{1,0},{2,1},{3,2},{4,3},{5,4},{6,5},{7,6},{8,7},{9,8},{10,9},{11,1... | collective-permute-start | bytes 786440 | tf_op jit(solution)/shard_map/ppermute | solution.py:20
  23.7 22.8 %copy-start.14 = (bf16[64,16,128]{2,0,1:T(8,128)(2,1)}, bf16[64,16,128]{2,0,1:T(8,128)(2,1)S(1)}, u32[]{:S(2)}) copy-start(bf16[64,16,128]{2,0,1:T(8,128)(2,1)S(1)} %collective-permute-done.1) | copy-start | bytes 786436
  25.8 10.9 %copy-start.19 = (bf16[3,3,64,64]{3,2,1,0:T(8,128)(2,1)S(1)}, bf16[3,3,64,64]{3,2,1,0:T(8,128)(2,1)}, u32[]{:S(2)}) copy-start(bf16[3,3,64,64]{3,2,1,0:T(8,128)(2,1)} %param.9) | copy-start | bytes 221188
  29.1 7.9 collective-permute-start.2
  35.2 7.4 collective-permute-start.3
  56.2 1.0 copy-start.10
  56.2 1.3 copy-start.12
  56.2 1.7 copy-start.7
  56.2 1.9 copy-start.9
  56.2 2.7 copy-start.3
  56.2 2.7 copy-start.5
  58.1 1.0 copy-start.15
  58.1 1.4 copy-start.17
  58.1 1.4 copy-start.27
  59.5 7.4 copy-start.26
  247.4 10.9 %copy-start.25 = (s32[2048]{0:T(1024)S(1)}, s32[2048]{0:T(1024)}, u32[]{:S(2)}) copy-start(s32[2048]{0:T(1024)} %param.15) | copy-start | bytes 24580
  251.9 33.7 %all-to-all-start.2 = ((bf16[62,32,128,2]{2,3,0,1:T(2,128)(2,1)}), bf16[62,32,128,2]{2,3,0,1:T(2,128)(2,1)}, u32[]{:S(2)}, u32[]{:S(2)}) async-start(bf16[62,32,128,2]{2,3,0,1:T(2,128)(2,1)} %copy.80), calls=%async_computation.2 | async-start | bytes 2031616 | tf_op jit(solution)/shard_map/all_to_all | solution.py:78
  258.2 617.8 %all-reduce.3.cloned.1.call-start = ((), (), s32[]{:S(2)}) async-start(), calls=%async_computation.3 | async-start | bytes 589824 | tf_op jit(solution)/shard_map/psum | solution.py:135
  288.3 4.6 copy-start.23
  290.6 2.6 copy-start.24
  294.4 2.0 copy-start.11
  294.4 2.0 copy-start.13
  296.4 111.1 %copy-start.8 = (bf16[64,64,128]{2,0,1:T(8,128)(2,1)S(1)}, bf16[64,64,128]{2,0,1:T(8,128)(2,1)}, u32[]{:S(2)}) copy-start(bf16[64,64,128]{2,0,1:T(8,128)(2,1)} %copy-done.7) | copy-start | bytes 3145732
  401.2 12.5 %collective-permute-start.4 = (bf16[64,16,128]{2,0,1:T(8,128)(2,1)}, bf16[64,16,128]{2,0,1:T(8,128)(2,1)}, u32[]{:S(2)}, u32[]{:S(2)}) collective-permute-start(bf16[64,16,128]{2,0,1:T(8,128)(2,1)} %get-tuple-element.51), channel_id=1, source_target_pairs={{0,1},{1,2},{2,3},{3,4},{4,5},{5,6},{6,7},{7,8},{8,9},{9,10},{10,1... | collective-permute-start | bytes 786440 | tf_op jit(solution)/shard_map/ppermute | solution.py:18
  405.5 5.3 copy-start.4
  405.5 5.3 copy-start.6
  405.5 5.3 copy-start.16
  405.5 8.8 collective-permute-start.5
  410.8 1.0 copy-start.20
  420.4 458.1 %collective-permute-start.6 = (bf16[64,96,16]{1,2,0:T(8,128)(2,1)S(1)}, bf16[64,96,16]{1,2,0:T(8,128)(2,1)S(1)}, u32[]{:S(2)}, u32[]{:S(2)}) collective-permute-start(bf16[64,96,16]{1,2,0:T(8,128)(2,1)S(1)} %copy.83), channel_id=1, source_target_pairs={{0,32},{32,64},{64,96},{96,128},{128,160},{160,192},{192,224},{224... | collective-permute-start | bytes 589832 | tf_op jit(solution)/shard_map/ppermute | solution.py:18
  425.2 456.5 %collective-permute-start.7 = (bf16[64,96,16]{1,2,0:T(8,128)(2,1)S(1)}, bf16[64,96,16]{1,2,0:T(8,128)(2,1)S(1)}, u32[]{:S(2)}, u32[]{:S(2)}) collective-permute-start(bf16[64,96,16]{1,2,0:T(8,128)(2,1)S(1)} %copy.85), channel_id=1, source_target_pairs={{32,0},{64,32},{96,64},{128,96},{160,128},{192,160},{224,192},{256... | collective-permute-start | bytes 589832 | tf_op jit(solution)/shard_map/ppermute | solution.py:20
  890.1 1.0 copy-start.22
  891.2 0.9 copy-start.21
  892.1 1.9 copy-start.2
  892.1 1.9 copy-start.18
  894.1 4.3 copy-start.1
Sparse Core Ops, SparseCore 0:
  412.6 463.3 all-reduce.2
where the time goes:
time: 910 us; the launch traced here: 905 us
  waiting for transfers between devices  481 us (53%)
  blocking collectives  227 us (25%)
  local copies, waits for them, and re-layouts  96.4 us (11%)
  starting transfers between devices  31.4 us (3%)
  other arithmetic  31.1 us (3%)
  matrix products  23.1 us (3%)
  between operations  14.9 us (2%)
    psum x1, waiting for transfers between devices, per_device(): lax.psum((conv_w_term, conv_b_term, head_w_term, head_b_term), ('row', 'c...  450 us
    psum x1, blocking collectives, per_device(): lax.psum((conv_w_term, conv_b_term, head_w_term, head_b_term), ('row', 'c...  100 us
    all_to_all x1, blocking collectives, mirror(): lax.all_to_all(lax.all_to_all(sectioned, 'col', split_axis=3, concat_axis...  90.6 us
    all_to_all x1, blocking collectives, mirror(): lax.all_to_all(sectioned, 'col', split_axis=3, concat_axis=1, tiled=True)  36.5 us
    unnamed x62, local copies, waits for them, and re-layouts  34.1 us
    all_to_all x1, waiting for transfers between devices, mirror(): lax.all_to_all(ordered, 'col', split_axis=1, concat_axis=3, tiled=True)  24.9 us
  transfers between devices with their start and end apart: 10, of which 5 were waited for; matrix products, arithmetic and copies ran while one was open for 3% of the time, Pallas kernels for 0%

commit v1 on v0

--- a/solution.py
+++ b/solution.py
@@ -1,10 +1,232 @@
 import jax
 import jax.numpy as jnp
 from jax import lax
+from jax.experimental import pallas as pl
+from jax.experimental.pallas import tpu as pltpu
 from jax.sharding import PartitionSpec as P
 
 DILATION_STEP = 16
 DB = 37
+
+MESH = pl.DeviceIdType.MESH
+
+
+def place():
+    row = lax.axis_index("row")
+    col = lax.axis_index("col")
+    x = lax.rem(row, 4)
+    zh = row // 4
+    core = lax.rem(col, 2)
+    q = col // 2
+    y = q // 4
+    zl = lax.rem(q, 4)
+    return x, y, 4 * zh + zl, core
+
+
+def device(x, y, z, core):
+    return ((z // 4) * 4 + x, (y * 4 + lax.rem(z, 4)) * 2 + core)
+
+
+def mirror_kernel(src, dst, tmp, send_a, recv_a, send_b, recv_b):
+    x, y, z, core = place()
+    me_k = 4 * y + x
+    a_target = lambda k: (lax.rem(k, 4), k // 4, z, core)
+    a_source = lambda s: (lax.rem(s, 4), s // 4, z, core)
+    a_slot = me_k
+    b_target = lambda s, h: (lax.rem(z, 4), z // 4, s, h)
+    b_source = lambda k, c: (lax.rem(k, 4), k // 4, me_k, c)
+    rot = me_k
+
+    def is_me(t):
+        return (t[0] == x) & (t[1] == y) & (t[2] == z) & (t[3] == core)
+
+    barrier = pltpu.get_barrier_semaphore()
+
+    def greet(t):
+        @pl.when(jnp.logical_not(is_me(t)))
+        def _():
+            pl.semaphore_signal(barrier, inc=1, device_id=device(*t), device_id_type=MESH)
+
+    def greet_all(s, carry):
+        greet(a_source(s))
+        greet(b_source(s, 0))
+        greet(b_source(s, 1))
+        return carry
+
+    lax.fori_loop(0, 16, greet_all, 0)
+
+    pl.semaphore_wait(barrier, jnp.where(me_k == z, 46, 47))
+
+    def phase_a(t, carry):
+        k = lax.rem(me_k + t, 16)
+        to = a_target(k)
+        for h in range(2):
+            @pl.when(is_me(to))
+            def _():
+                pltpu.make_async_copy(src.at[h, k], tmp.at[a_slot, h], recv_a.at[a_slot, h]).start()
+
+            @pl.when(jnp.logical_not(is_me(to)))
+            def _():
+                pltpu.make_async_remote_copy(
+                    src_ref=src.at[h, k], dst_ref=tmp.at[a_slot, h], send_sem=send_a.at[k, h],
+                    recv_sem=recv_a.at[a_slot, h], device_id=device(*to), device_id_type=MESH).start()
+        return carry
+
+    lax.fori_loop(0, 16, phase_a, 0)
+
+    def phase_b(t, carry):
+        s = lax.rem(rot + t, 16)
+        for h in range(2):
+            pltpu.make_async_copy(src.at[h, 0], tmp.at[s, h], recv_a.at[s, h]).wait()
+            to = b_target(s, h)
+            @pl.when(is_me(to))
+            def _():
+                pltpu.make_async_copy(tmp.at[s, h], dst.at[core, me_k], recv_b.at[core, me_k]).start()
+
+            @pl.when(jnp.logical_not(is_me(to)))
+            def _():
+                pltpu.make_async_remote_copy(
+                    src_ref=tmp.at[s, h], dst_ref=dst.at[core, me_k], send_sem=send_b.at[s, h],
+                    recv_sem=recv_b.at[core, me_k], device_id=device(*to), device_id_type=MESH).start()
+        return carry
+
+    lax.fori_loop(0, 16, phase_b, 0)
+
+    def finish(k, carry):
+        for c in range(2):
+            pltpu.make_async_copy(tmp.at[0, 0], dst.at[c, k], recv_b.at[c, k]).wait()
+        for h in range(2):
+            @pl.when(jnp.logical_not(is_me(a_target(k))))
+            def _():
+                pltpu.make_async_copy(src.at[h, k], tmp.at[0, h], send_a.at[k, h]).wait()
+
+            @pl.when(jnp.logical_not(is_me(b_target(k, h))))
+            def _():
+                pltpu.make_async_copy(tmp.at[k, h], dst.at[0, 0], send_b.at[k, h]).wait()
+        return carry
+
+    lax.fori_loop(0, 16, finish, 0)
+
+
+def exchange(packed):
+    piece = packed.shape[2:]
+    return pl.pallas_call(
+        mirror_kernel,
+        out_shape=jax.ShapeDtypeStruct(packed.shape, packed.dtype),
+        in_specs=[pl.BlockSpec(memory_space=pltpu.VMEM)],
+        out_specs=pl.BlockSpec(memory_space=pltpu.VMEM),
+        scratch_shapes=[
+            pltpu.VMEM((16, 2) + piece, packed.dtype),
+            pltpu.SemaphoreType.DMA((16, 2)),
+            pltpu.SemaphoreType.DMA((16, 2)),
+            pltpu.SemaphoreType.DMA((16, 2)),
+            pltpu.SemaphoreType.DMA((2, 16)),
+        ],
+        compiler_params=pltpu.CompilerParams(collective_id=1, has_side_effects=True),
+        name="mirror",
+    )(packed)
+
+
+def total_kernel(src, dst, parts, mine, ring, send_1, recv_1, send_2, recv_2, send_3, recv_3):
+    x, y, z, core = place()
+    me_s = (4 * y + x) * 2 + core
+
+    def plane(s):
+        return (lax.rem(s // 2, 4), s // 8, z, lax.rem(s, 2))
+
+    barrier = pltpu.get_barrier_semaphore()
+
+    def greet_plane(t, carry):
+        s = lax.rem(me_s + t, 32)
+        pl.semaphore_signal(barrier, inc=1, device_id=device(*plane(s)), device_id_type=MESH)
+        return carry
+
+    def greet_ring(t, carry):
+        pl.semaphore_signal(
+            barrier, inc=1, device_id=device(x, y, lax.rem(z + t, 16), core), device_id_type=MESH)
+        return carry
+
+    lax.fori_loop(1, 32, greet_plane, 0)
+    lax.fori_loop(1, 16, greet_ring, 0)
+    pl.semaphore_wait(barrier, 46)
+
+    def send_parts(t, carry):
+        s = lax.rem(me_s + t, 32)
+        pltpu.make_async_remote_copy(
+            src_ref=src.at[s], dst_ref=parts.at[me_s], send_sem=send_1.at[s],
+            recv_sem=recv_1.at[me_s], device_id=device(*plane(s)), device_id_type=MESH).start()
+        return carry
+
+    lax.fori_loop(1, 32, send_parts, 0)
+
+    def wait_parts(t, carry):
+        s = lax.rem(me_s + t, 32)
+        pltpu.make_async_copy(src.at[0], parts.at[s], recv_1.at[s]).wait()
+        return carry
+
+    parts[me_s] = src[me_s]
+    lax.fori_loop(1, 32, wait_parts, 0)
+    mine[...] = jnp.sum(parts[...], axis=0)
+    ring[z] = mine[...]
+
+    def send_ring(t, carry):
+        o = lax.rem(z + t, 16)
+        pltpu.make_async_remote_copy(
+            src_ref=mine, dst_ref=ring.at[z], send_sem=send_2.at[o],
+            recv_sem=recv_2.at[z], device_id=device(x, y, o, core), device_id_type=MESH).start()
+        return carry
+
+    lax.fori_loop(1, 16, send_ring, 0)
+
+    def wait_ring(t, carry):
+        o = lax.rem(z + t, 16)
+        pltpu.make_async_copy(mine, ring.at[o], recv_2.at[o]).wait()
+        pltpu.make_async_copy(mine, ring.at[o], send_2.at[o]).wait()
+        return carry
+
+    lax.fori_loop(1, 16, wait_ring, 0)
+    mine[...] = jnp.sum(ring[...], axis=0)
+    dst[me_s] = mine[...]
+
+    def send_all(t, carry):
+        s = lax.rem(me_s + t, 32)
+        pltpu.make_async_remote_copy(
+            src_ref=mine, dst_ref=dst.at[me_s], send_sem=send_3.at[s],
+            recv_sem=recv_3.at[me_s], device_id=device(*plane(s)), device_id_type=MESH).start()
+        return carry
+
+    lax.fori_loop(1, 32, send_all, 0)
+
+    def finish(t, carry):
+        s = lax.rem(me_s + t, 32)
+        pltpu.make_async_copy(mine, dst.at[s], recv_3.at[s]).wait()
+        pltpu.make_async_copy(mine, dst.at[s], send_3.at[s]).wait()
+        pltpu.make_async_copy(mine, dst.at[s], send_1.at[s]).wait()
+        return carry
+
+    lax.fori_loop(1, 32, finish, 0)
+
+
+def total(values):
+    return pl.pallas_call(
+        total_kernel,
+        out_shape=jax.ShapeDtypeStruct(values.shape, values.dtype),
+        in_specs=[pl.BlockSpec(memory_space=pltpu.VMEM)],
+        out_specs=pl.BlockSpec(memory_space=pltpu.VMEM),
+        scratch_shapes=[
+            pltpu.VMEM(values.shape, values.dtype),
+            pltpu.VMEM(values.shape[1:], values.dtype),
+            pltpu.VMEM((16,) + values.shape[1:], values.dtype),
+            pltpu.SemaphoreType.DMA((32,)),
+            pltpu.SemaphoreType.DMA((32,)),
+            pltpu.SemaphoreType.DMA((16,)),
+            pltpu.SemaphoreType.DMA((16,)),
+            pltpu.SemaphoreType.DMA((32,)),
+            pltpu.SemaphoreType.DMA((32,)),
+        ],
+        compiler_params=pltpu.CompilerParams(collective_id=2, has_side_effects=True),
+        name="total",
+    )(values)
 
 
 def with_halo(cells, sides, width):
@@ -62,21 +284,10 @@
 
 def mirror(logits):
     bins, row_span, column_span = logits.shape
-    ncol = lax.axis_size("col")
-    nrow = lax.axis_size("row")
-    ratio = ncol // nrow
-    piece = row_span // ncol
-    sectioned = logits.reshape(bins, row_span, ratio, ncol, piece)
-    moved = lax.all_to_all(
-        lax.all_to_all(sectioned, "col", split_axis=3, concat_axis=1, tiled=True),
-        "row",
-        split_axis=1,
-        concat_axis=3,
-        tiled=True,
-    )
-    ordered = jnp.transpose(moved, (0, 3, 2, 1, 4)).reshape(bins, ncol, column_span, piece)
-    placed = lax.all_to_all(ordered, "col", split_axis=1, concat_axis=3, tiled=True)
-    return jnp.transpose(placed.reshape(bins, column_span, row_span), (0, 2, 1))
+    padded = jnp.pad(logits, ((0, 64 - bins), (0, 0), (0, 0)))
+    packed = jnp.transpose(padded.reshape(2, 32, row_span, 2, 64), (3, 1, 2, 0, 4))
+    placed = exchange(packed.reshape(2, 16, 2, row_span, 128)).reshape(2, 32, row_span, 2, 64)
+    return jnp.transpose(placed, (3, 1, 4, 0, 2)).reshape(64, row_span, column_span)[:bins]
 
 
 def group_grad(scores, labels):
@@ -132,9 +343,15 @@
         tap_rows.append(jnp.transpose(flat.reshape(channels, 3, channels), (1, 0, 2)))
     conv_w_term = jnp.stack(tap_rows, 0)
     conv_b_term = jnp.sum(grad_mixed, axis=(1, 2))
-    conv_w_sum, conv_b_sum, head_w_sum, head_b_sum = lax.psum(
-        (conv_w_term, conv_b_term, head_w_term, head_b_term), ("row", "col")
-    )
+    flat = jnp.concatenate(
+        [conv_w_term.reshape(-1), head_w_term.reshape(-1), conv_b_term, head_b_term]
+    )
+    flat = jnp.pad(flat, (0, 40960 - flat.shape[0]))
+    summed = total(flat.reshape(32, 10, 128)).reshape(-1)
+    conv_w_sum = summed[:36864].reshape(conv_w_term.shape)
+    head_w_sum = summed[36864:40832].reshape(head_w_term.shape)
+    conv_b_sum = summed[40832:40896]
+    head_b_sum = summed[40896:40958]
     slope = jnp.where(x32 > 0.0, jnp.float32(1.0), jnp.exp(jnp.minimum(x32, 0.0)))
     grad_input = (grad_mixed + slope * grad_act).astype(jnp.bfloat16)
     return (

time: 910 us -> 350 us (0.38)
  the two profiles are of different devices: /device:TPU:1 before, /device:TPU:15 now
where the time goes in v1:
time: 350 us; the launch traced here: 346 us
  Pallas kernels  111 us (32%)
  local copies, waits for them, and re-layouts  84.3 us (24%)
  waiting for transfers between devices  61.4 us (18%)
  starting transfers between devices  31 us (9%)
  other arithmetic  29.6 us (8%)
  matrix products  26.7 us (8%)
    pallas_call x1, Pallas kernels, exchange(): pl.pallas_call(mirror_kernel, out_shape=jax.ShapeDtypeStruct(packed.shape...  70.1 us
    ppermute x4, waiting for transfers between devices, with_halo(): lax.ppermute(head, axis, [((i + 1) % count, i) for i in range(ends)])  59.8 us
    pallas_call x1, Pallas kernels, total(): pl.pallas_call(total_kernel, out_shape=jax.ShapeDtypeStruct(values.shape,...  40.8 us
    ppermute x4, starting transfers between devices, with_halo(): lax.ppermute(tail, axis, [(i, (i + 1) % count) for i in range(ends)])  22.9 us
    dot_general x6, matrix products, dilated(): jnp.einsum('ok,kxy->oxy', tap_matrix(weight, first_member), stacked, pref...  18.3 us
    reshape x2, local copies, waits for them, and re-layouts, mirror(): padded.reshape(2, 32, row_span, 2, 64)  18.2 us
    concatenate x4, other arithmetic, with_halo(): jnp.concatenate([lax.ppermute(tail, axis, [(i, (i + 1) % count) for i in...  16.3 us
    slice x4, local copies, waits for them, and re-layouts, with_halo(): lax.slice_in_dim(cells, cells.shape[dim] - width, cells.shape[dim], axis=...  9.5 us
  transfers between devices with their start and end apart: 8, of which 5 were waited for; matrix products, arithmetic and copies ran while one was open for 6% of the time, Pallas kernels for 0%

profile of v1, /device:TPU:15, one launch (start us, length us, event | category | flops | bytes accessed | tf_op | source)
XLA Modules:
  0.0 345.5 jit_solution(11833267790048803428)
XLA Ops:
  0.7 2.4 fusion.31
  3.1 4.1 %collective-permute-start = (bf16[64,16,128]{2,0,1:T(8,128)(2,1)S(1)}, bf16[64,16,128]{2,0,1:T(8,128)(2,1)S(1)}, u32[]{:S(2)}, u32[]{:S(2)}) collective-permute-start(bf16[64,16,128]{2,0,1:T(8,128)(2,1)S(1)} %get-tuple-element.45), channel_id=1, source_target_pairs={{0,1},{1,2},{2,3},{3,4},{4,5},{5,6},{6,7},{7,8},{8,9},{9,10},{10,1... | collective-permute-start | bytes 786440 | tf_op jit(solution)/shard_map/ppermute | solution.py:240
  7.2 1.9 collective-permute-start.1
  12.8 3.6 %collective-permute-done.1 = bf16[64,16,128]{2,0,1:T(8,128)(2,1)S(1)} collective-permute-done((bf16[64,16,128]{2,0,1:T(8,128)(2,1)S(1)}, bf16[64,16,128]{2,0,1:T(8,128)(2,1)S(1)}, u32[]{:S(2)}, u32[]{:S(2)}) %collective-permute-start.1) | collective-permute-done | bytes 262176 | tf_op jit(solution)/shard_map/ppermute | solution.py:242
  16.6 1.8 fusion.74
  18.4 2.6 copy.43
  21.1 8.7 %collective-permute-start.2 = (bf16[64,96,16]{1,2,0:T(8,128)(2,1)S(1)}, bf16[64,96,16]{1,2,0:T(8,128)(2,1)}, u32[]{:S(2)}, u32[]{:S(2)}) collective-permute-start(bf16[64,96,16]{1,2,0:T(8,128)(2,1)S(1)} %copy.43), channel_id=1, source_target_pairs={{0,32},{32,64},{64,96},{96,128},{128,160},{160,192},{192,224},{224... | collective-permute-start | bytes 589832 | tf_op jit(solution)/shard_map/ppermute | solution.py:240
  29.8 2.3 copy.45
  32.1 2.3 collective-permute-start.3
  34.5 1.6 collective-permute-done.2
  36.1 3.1 copy.44
  39.2 26.3 %collective-permute-done.3 = bf16[64,96,16]{1,2,0:T(8,128)(2,1)} collective-permute-done((bf16[64,96,16]{1,2,0:T(8,128)(2,1)}, bf16[64,96,16]{1,2,0:T(8,128)(2,1)}, u32[]{:S(2)}, u32[]{:S(2)}) %collective-permute-start.3) | collective-permute-done | bytes 196640 | tf_op jit(solution)/shard_map/ppermute | solution.py:242
  65.5 3.9 %copy.46 = bf16[64,96,16]{2,0,1:T(8,128)(2,1)} copy(bf16[64,96,16]{1,2,0:T(8,128)(2,1)} %collective-permute-done.3) | data formatting | bytes 393216 | tf_op jit(solution)/shard_map/ppermute | solution.py:242
  69.4 7.9 %maximum_maximum_fusion = (bf16[64,96,144]{2,0,1:T(8,128)(2,1)S(1)}, bf16[64,96,144]{2,0,1:T(8,128)(2,1)S(1)}) fusion(bf16[64,16,128]{2,0,1:T(8,128)(2,1)S(1)} %collective-permute-done.1, bf16[64,64,128]{2,0,1:T(8,128)(2,1)S(1)} %fusion.31, bf16[64,16,128]{2,0,1:T(8,128)(2,1)S(1)} %collective-permute-done, bf16[64,96,16]{2,0,1:T(8,128)(2,1)S(1)} %copy.44, ...), kind=kLoop, calls=%fused_computation.24 | loop fusion | flops 14155776 | bytes 5505024 | tf_op jit(solution)/shard_map/concatenate | solution.py:238
  77.3 1.8 fusion.70
  82.3 7.4 %fusion.32 = bf16[64,64,128]{2,0,1:T(8,128)(2,1)S(1)} fusion(f32[64,128,64]{1,2,0:T(8,128)S(1)} %fusion.47, f32[64,128,64]{1,2,0:T(8,128)S(1)} %fusion.42, bf16[64,192,1]{0,1,2:T(8,128)(2,1)S(1)} %bitcast.117, f32[64]{0:T(128)S(1)} %copy-done.33, bf16[64,64,128]{2,1,0:T(8,128)(2,1)S(1)} %copy-done.18, bf16[64,16,128]{2,0,1:T(8,128)(2,1)S(1)} %collective-permute-done.1, ...), kind=kOutput, calls=%fused_computation.44 | convolution fusion | flops 217055232 | bytes 9724160 | tf_op jit(solution)/shard_map/ok,kxy->oxy/dot_general | solution.py:275
  91.3 13.1 %reshape.105 = bf16[2,32,64,2,64]{4,3,1,0,2:T(2,128)(2,1)} reshape(bf16[64,64,128]{2,0,1:T(8,128)(2,1)S(1)} %pad.8) | data formatting | bytes 2097152 | tf_op jit(solution)/shard_map/reshape | solution.py:288
  104.4 5.1 %copy.92 = bf16[2,32,64,2,64]{4,0,2,1,3:T(2,128)(2,1)} copy(bf16[2,32,64,2,64]{4,3,1,0,2:T(2,128)(2,1)} %reshape.105) | data formatting | bytes 2097152 | tf_op jit(solution)/shard_map/reshape | solution.py:288
  109.5 4.7 %reshape.106.src = bf16[2,16,2,64,128]{4,3,2,1,0:T(8,128)(2,1)} reshape(bf16[2,32,64,2,64]{4,3,2,1,0:T(2,128)(2,1)} %bitcast.107) | data formatting | bytes 2097152 | tf_op jit(solution)/shard_map/reshape | solution.py:289
  114.2 70.1 %mirror.1 = bf16[2,16,2,64,128]{4,3,2,1,0:T(8,128)(2,1)} custom-call(bf16[2,16,2,64,128]{4,3,2,1,0:T(8,128)(2,1)} %reshape.106.src), custom_call_target="tpu_custom_call" | custom-call | tf_op jit(solution)/shard_map/mirror/pallas_call | solution.py:113
  184.4 5.0 %reshape.107 = bf16[2,32,64,2,64]{4,3,2,1,0:T(2,128)(2,1)} reshape(bf16[2,16,2,64,128]{4,3,2,1,0:T(8,128)(2,1)} %mirror.1) | data formatting | bytes 2097152 | tf_op jit(solution)/shard_map/reshape | solution.py:289
  189.3 8.0 %copy.54 = bf16[2,32,64,2,64]{4,3,1,0,2:T(2,128)(2,1)} copy(bf16[2,32,64,2,64]{2,0,4,1,3:T(2,128)(2,1)} %bitcast.108) | data formatting | bytes 2097152 | tf_op jit(solution)/shard_map/transpose | solution.py:290
  197.3 3.9 %reshape.108 = bf16[64,64,128]{2,0,1:T(8,128)(2,1)S(1)} reshape(bf16[2,32,64,2,64]{4,3,1,0,2:T(2,128)(2,1)} %copy.54) | data formatting | bytes 2097152 | tf_op jit(solution)/shard_map/reshape | solution.py:290
  201.7 2.3 fusion.79
  204.0 2.3 fusion.78
  208.0 2.0 fusion.72
  210.0 1.6 fusion.41
  212.5 3.0 fusion.45
  217.7 40.8 %total.1 = f32[32,10,128]{2,1,0:T(8,128)} custom-call(f32[32,10,128]{2,1,0:T(8,128)} %reshape.117.src), custom_call_target="tpu_custom_call" | custom-call | tf_op jit(solution)/shard_map/total/pallas_call | solution.py:211
  259.5 2.4 collective-permute-start.4
  261.9 1.9 collective-permute-start.5
  264.5 1.2 slice_divide_fusion.2
  265.7 1.1 slice.209
  267.6 1.2 slice_divide_fusion.1
  268.8 3.0 collective-permute-done.5
  272.0 2.4 fusion.73
  274.4 2.6 copy.56
  277.0 7.7 %collective-permute-start.6 = (bf16[64,96,16]{1,2,0:T(8,128)(2,1)S(1)}, bf16[64,96,16]{1,2,0:T(8,128)(2,1)S(1)}, u32[]{:S(2)}, u32[]{:S(2)}) collective-permute-start(bf16[64,96,16]{1,2,0:T(8,128)(2,1)S(1)} %copy.56), channel_id=1, source_target_pairs={{0,32},{32,64},{64,96},{96,128},{128,160},{160,192},{192,224},{224... | collective-permute-start | bytes 589832 | tf_op jit(solution)/shard_map/ppermute | solution.py:240
  284.7 2.7 copy.58
  287.4 1.9 collective-permute-start.7
  289.3 1.1 slice_divide_fusion.3
  290.4 3.0 copy.57
  293.5 26.9 %collective-permute-done.7 = bf16[64,96,16]{1,2,0:T(8,128)(2,1)S(1)} collective-permute-done((bf16[64,96,16]{1,2,0:T(8,128)(2,1)S(1)}, bf16[64,96,16]{1,2,0:T(8,128)(2,1)S(1)}, u32[]{:S(2)}, u32[]{:S(2)}) %collective-permute-start.7) | collective-permute-done | bytes 196640 | tf_op jit(solution)/shard_map/ppermute | solution.py:242
  320.3 3.0 copy.59
  323.4 8.0 %maximum_maximum_fusion.1 = (bf16[64,96,144]{2,0,1:T(8,128)(2,1)S(1)}, bf16[64,96,144]{2,0,1:T(8,128)(2,1)S(1)}) fusion(bf16[64,16,128]{2,0,1:T(8,128)(2,1)S(1)} %collective-permute-done.5, bf16[64,64,128]{2,0,1:T(8,128)(2,1)S(1)} %get-tuple-element.33, bf16[64,16,128]{2,0,1:T(8,128)(2,1)S(1)} %collective-permute-done.4, bf16[64,96,16]{2,0,1:T(8,128)(2,1)} %copy.57, ...), kind=kLoop, calls=%fused_computation.27 | loop fusion | flops 14155776 | bytes 5505024 | tf_op jit(solution)/shard_map/concatenate | solution.py:238
  332.2 1.0 fusion.69
  336.1 7.6 %fusion.29 = bf16[64,64,128]{2,0,1:T(8,128)(2,1)S(1)} fusion(f32[64,128,64]{1,2,0:T(8,128)S(1)} %copy-done.4, f32[64,128,64]{1,2,0:T(8,128)S(1)} %fusion.10, f32[64,128,64]{1,2,0:T(8,128)S(1)} %fusion.19, bf16[64,64,128]{2,1,0:T(8,128)(2,1)S(1)} %copy-done.19, bf16[64,192,1]{0,1,2:T(8,128)(2,1)S(1)} %bitcast.112, ...), kind=kOutput, calls=%fused_computation.41 | convolution fusion | flops 218628096 | bytes 11821056 | tf_op jit(solution)/shard_map/ok,kxy->oxy/dot_general | solution.py:275
  343.6 1.6 copy.67
  (109 shorter events, 19.8 us)
Async XLA Ops:
  0.6 90.1 %copy-start = (bf16[62,64]{1,0:T(8,128)(2,1)S(1)}, bf16[62,64]{1,0:T(8,128)(2,1)}, u32[]{:S(2)}) copy-start(bf16[62,64]{1,0:T(8,128)(2,1)} %param.11) | copy-start | bytes 23812
  0.6 8.5 %copy-start.20 = (bf16[3,3,64,64]{3,2,1,0:T(8,128)(2,1)S(1)}, bf16[3,3,64,64]{3,2,1,0:T(8,128)(2,1)}, u32[]{:S(2)}) copy-start(bf16[3,3,64,64]{3,2,1,0:T(8,128)(2,1)} %param.9) | copy-start | bytes 221188
  0.7 8.5 %copy-start.31 = (s32[2048]{0:T(1024)S(1)}, s32[2048]{0:T(1024)}, u32[]{:S(2)}) copy-start(s32[2048]{0:T(1024)} %param.15) | copy-start | bytes 24580
  3.1 9.7 %collective-permute-start = (bf16[64,16,128]{2,0,1:T(8,128)(2,1)S(1)}, bf16[64,16,128]{2,0,1:T(8,128)(2,1)S(1)}, u32[]{:S(2)}, u32[]{:S(2)}) collective-permute-start(bf16[64,16,128]{2,0,1:T(8,128)(2,1)S(1)} %get-tuple-element.45), channel_id=1, source_target_pairs={{0,1},{1,2},{2,3},{3,4},{4,5},{5,6},{6,7},{7,8},{8,9},{9,10},{10,1... | collective-permute-start | bytes 786440 | tf_op jit(solution)/shard_map/ppermute | solution.py:240
  7.2 9.2 %collective-permute-start.1 = (bf16[64,16,128]{2,0,1:T(8,128)(2,1)S(1)}, bf16[64,16,128]{2,0,1:T(8,128)(2,1)S(1)}, u32[]{:S(2)}, u32[]{:S(2)}) collective-permute-start(bf16[64,16,128]{2,0,1:T(8,128)(2,1)S(1)} %get-tuple-element.44), channel_id=1, source_target_pairs={{1,0},{2,1},{3,2},{4,3},{5,4},{6,5},{7,6},{8,7},{9,8},{10,9},{11,1... | collective-permute-start | bytes 786440 | tf_op jit(solution)/shard_map/ppermute | solution.py:242
  16.4 65.4 %copy-start.16 = (bf16[64,16,128]{2,0,1:T(8,128)(2,1)}, bf16[64,16,128]{2,0,1:T(8,128)(2,1)S(1)}, u32[]{:S(2)}) copy-start(bf16[64,16,128]{2,0,1:T(8,128)(2,1)S(1)} %collective-permute-done.1) | copy-start | bytes 786436
  21.1 15.0 %collective-permute-start.2 = (bf16[64,96,16]{1,2,0:T(8,128)(2,1)S(1)}, bf16[64,96,16]{1,2,0:T(8,128)(2,1)}, u32[]{:S(2)}, u32[]{:S(2)}) collective-permute-start(bf16[64,96,16]{1,2,0:T(8,128)(2,1)S(1)} %copy.43), channel_id=1, source_target_pairs={{0,32},{32,64},{64,96},{96,128},{128,160},{160,192},{192,224},{224... | collective-permute-start | bytes 589832 | tf_op jit(solution)/shard_map/ppermute | solution.py:240
  32.1 33.4 %collective-permute-start.3 = (bf16[64,96,16]{1,2,0:T(8,128)(2,1)}, bf16[64,96,16]{1,2,0:T(8,128)(2,1)}, u32[]{:S(2)}, u32[]{:S(2)}) collective-permute-start(bf16[64,96,16]{1,2,0:T(8,128)(2,1)} %copy.45), channel_id=1, source_target_pairs={{32,0},{64,32},{96,64},{128,96},{160,128},{192,160},{224,192},{256... | collective-permute-start | bytes 589832 | tf_op jit(solution)/shard_map/ppermute | solution.py:242
  77.2 1.8 copy-start.26
  79.0 1.0 copy-start.12
  79.0 1.4 copy-start.14
  79.0 1.7 copy-start.9
  79.1 2.0 copy-start.11
  79.1 2.7 copy-start.5
  79.1 2.7 copy-start.7
  79.1 1.9 copy-start.27
  81.0 1.3 copy-start.18
  81.0 1.3 copy-start.28
  81.0 1.3 copy-start.33
  82.3 8.4 %copy-start.32 = (f32[62]{0:T(128)S(1)}, f32[62]{0:T(128)}, u32[]{:S(2)}) copy-start(f32[62]{0:T(128)} %param.12) | copy-start | bytes 748
  89.7 1.0 copy-start.2
  201.6 4.6 %copy-start.29 = (s32[64,128]{1,0:T(8,128)S(1)}, s32[64,128]{1,0:T(8,128)}, u32[]{:S(2)}) copy-start(s32[64,128]{1,0:T(8,128)} %param.13) | copy-start | bytes 98308
  204.0 2.6 copy-start.30
  206.3 1.2 copy-start.3
  208.0 2.0 copy-start.13
  208.0 2.0 copy-start.15
  210.0 2.5 copy-start.10
  212.5 3.0 copy-start.6
  212.5 3.0 copy-start.8
  212.5 3.0 copy-start.17
  215.6 1.0 copy-start.23
  216.5 43.0 %copy-start.22 = (bf16[64,16,128]{2,0,1:T(8,128)(2,1)S(1)}, bf16[64,16,128]{2,0,1:T(8,128)(2,1)}, u32[]{:S(2)}) copy-start(bf16[64,16,128]{2,0,1:T(8,128)(2,1)} %get-tuple-element.43) | copy-start | bytes 786436
  216.5 45.4 %copy-start.21 = (bf16[64,16,128]{2,0,1:T(8,128)(2,1)S(1)}, bf16[64,16,128]{2,0,1:T(8,128)(2,1)}, u32[]{:S(2)}) copy-start(bf16[64,16,128]{2,0,1:T(8,128)(2,1)} %get-tuple-element.42) | copy-start | bytes 786436
  259.5 9.3 %collective-permute-start.4 = (bf16[64,16,128]{2,0,1:T(8,128)(2,1)S(1)}, bf16[64,16,128]{2,0,1:T(8,128)(2,1)S(1)}, u32[]{:S(2)}, u32[]{:S(2)}) collective-permute-start(bf16[64,16,128]{2,0,1:T(8,128)(2,1)S(1)} %copy-done.22), channel_id=1, source_target_pairs={{0,1},{1,2},{2,3},{3,4},{4,5},{5,6},{6,7},{7,8},{8,9},{9,10},{10,1... | collective-permute-start | bytes 786440 | tf_op jit(solution)/shard_map/ppermute | solution.py:240
  261.9 9.9 %collective-permute-start.5 = (bf16[64,16,128]{2,0,1:T(8,128)(2,1)S(1)}, bf16[64,16,128]{2,0,1:T(8,128)(2,1)S(1)}, u32[]{:S(2)}, u32[]{:S(2)}) collective-permute-start(bf16[64,16,128]{2,0,1:T(8,128)(2,1)S(1)} %copy-done.21), channel_id=1, source_target_pairs={{1,0},{2,1},{3,2},{4,3},{5,4},{6,5},{7,6},{8,7},{9,8},{10,9},{11,1... | collective-permute-start | bytes 786440 | tf_op jit(solution)/shard_map/ppermute | solution.py:242
  277.0 13.4 %collective-permute-start.6 = (bf16[64,96,16]{1,2,0:T(8,128)(2,1)S(1)}, bf16[64,96,16]{1,2,0:T(8,128)(2,1)S(1)}, u32[]{:S(2)}, u32[]{:S(2)}) collective-permute-start(bf16[64,96,16]{1,2,0:T(8,128)(2,1)S(1)} %copy.56), channel_id=1, source_target_pairs={{0,32},{32,64},{64,96},{96,128},{128,160},{160,192},{192,224},{224... | collective-permute-start | bytes 589832 | tf_op jit(solution)/shard_map/ppermute | solution.py:240
  287.4 33.0 %collective-permute-start.7 = (bf16[64,96,16]{1,2,0:T(8,128)(2,1)S(1)}, bf16[64,96,16]{1,2,0:T(8,128)(2,1)S(1)}, u32[]{:S(2)}, u32[]{:S(2)}) collective-permute-start(bf16[64,96,16]{1,2,0:T(8,128)(2,1)S(1)} %copy.58), channel_id=1, source_target_pairs={{32,0},{64,32},{96,64},{128,96},{160,128},{192,160},{224,192},{256... | collective-permute-start | bytes 589832 | tf_op jit(solution)/shard_map/ppermute | solution.py:242
  332.2 1.0 copy-start.25
  333.3 1.0 copy-start.24
  334.2 1.6 copy-start.4
  334.2 1.8 copy-start.19
  336.1 9.2 %copy-start.1 = (bf16[62,64]{1,0:T(8,128)(2,1)S(1)}, bf16[62,64]{1,0:T(8,128)(2,1)}, u32[]{:S(2)}) copy-start(bf16[62,64]{1,0:T(8,128)(2,1)} %param.11) | copy-start | bytes 23812

commit v2 on v0

v2 whole, which is shorter than its diff:
```python
import functools

import jax
import jax.numpy as jnp
from jax import lax
from jax.experimental import pallas as pl
from jax.experimental.pallas import tpu as pltpu
from jax.sharding import PartitionSpec as P

MESH = pl.DeviceIdType.MESH
F32 = jnp.float32
BF16 = jnp.bfloat16
DB = 37
NB = 62

RIMS = (
    (0, 1, "own", 64, 16, "own", 0),
    (0, -1, "own", 16, 16, "own", 80),
    (1, 0, "right", 0, 8, "from_left", 2),
    (-1, 0, "left", 0, 8, "from_right", 2),
    (1, 1, "right", 6, 2, "from_left", 0),
    (1, -1, "right", 0, 2, "from_left", 10),
    (-1, 1, "left", 6, 2, "from_right", 0),
    (-1, -1, "left", 0, 2, "from_right", 10),
)


def device(x, y, z, core):
    return ((z // 4) * 4 + x, (y * 4 + lax.rem(z, 4)) * 2 + core)


class Place:
    def __init__(self):
        self.row = lax.axis_index("row")
        self.col = lax.axis_index("col")
        self.x = lax.rem(self.row, 4)
        self.core = lax.rem(self.col, 2)
        chip = self.col // 2
        self.y = chip // 4
        self.z = 4 * (self.row // 4) + lax.rem(chip, 4)
        self.spot = 4 * self.y + self.x

    def inside(self, row_step, col_step):
        row, col = self.row + row_step, self.col + col_step
        return (row >= 0) & (row < 16) & (col >= 0) & (col < 32)

    def is_me(self, t):
        return (t[0] == self.x) & (t[1] == self.y) & (t[2] == self.z) & (t[3] == self.core)

    def mirror_first(self, k):
        return (lax.rem(k, 4), k // 4, self.z, self.core)

    def mirror_second(self, s, half):
        return (lax.rem(self.z, 4), self.z // 4, s, half)

    def mirror_giver(self, k, core):
        return (lax.rem(k, 4), k // 4, self.spot, core)

    def plane(self, s):
        return (lax.rem(s // 2, 4), s // 8, self.z, lax.rem(s, 2))

    def plane_slot(self):
        return self.spot * 2 + self.core

    def ring(self, z):
        return (self.x, self.y, z, self.core)


def signal(barrier, target):
    pl.semaphore_signal(barrier, inc=1, device_id=target, device_id_type=MESH)


def greet(me, barrier):
    for row_step, col_step in [r[:2] for r in RIMS]:
        @pl.when(me.inside(row_step, col_step))
        def _():
            signal(barrier, (me.row + row_step, me.col + col_step))

    def mirror_partners(s, carry):
        for t in (me.mirror_first(s), me.mirror_giver(s, 0), me.mirror_giver(s, 1)):
            @pl.when(jnp.logical_not(me.is_me(t)))
            def _():
                signal(barrier, device(*t))
        return carry

    lax.fori_loop(0, 16, mirror_partners, 0)

    def plane_partners(t, carry):
        signal(barrier, device(*me.plane(lax.rem(me.plane_slot() + t, 32))))
        return carry

    lax.fori_loop(1, 32, plane_partners, 0)

    def ring_partners(t, carry):
        signal(barrier, device(*me.ring(lax.rem(me.z + t, 16))))
        return carry

    lax.fori_loop(1, 16, ring_partners, 0)


def await_greetings(me, barrier):
    rows = 3 - jnp.where(me.row == 0, 1, 0) - jnp.where(me.row == 15, 1, 0)
    cols = 3 - jnp.where(me.col == 0, 1, 0) - jnp.where(me.col == 31, 1, 0)
    others = 46 + 47 - jnp.where(me.spot == me.z, 1, 0)
    pl.semaphore_wait(barrier, rows * cols - 1 + others)


def rim_copy(me, refs, sems, at):
    row_step, col_step, source, first, many, target, into = RIMS[at]
    return pltpu.make_async_remote_copy(
        src_ref=refs[source].at[pl.ds(first, many)],
        dst_ref=refs[target].at[pl.ds(into, many)],
        send_sem=sems[0].at[at],
        recv_sem=sems[1].at[at],
        device_id=(me.row + row_step, me.col + col_step),
        device_id_type=MESH,
    )


def send_rims(me, refs, sems):
    for at, (row_step, col_step, _, _, many, target, into) in enumerate(RIMS):
        @pl.when(me.inside(row_step, col_step))
        def _():
            rim_copy(me, refs, sems, at).start()

        @pl.when(jnp.logical_not(me.inside(-row_step, -col_step)))
        def _():
            refs[target][into : into + many] = jnp.zeros((many, 64, 128), BF16)


def await_rims(me, refs, sems):
    for at, (row_step, col_step) in enumerate([r[:2] for r in RIMS]):
        @pl.when(me.inside(-row_step, -col_step))
        def _():
            rim_copy(me, refs, sems, at).wait_recv()


def await_sent_rims(me, refs, sems):
    for at, (row_step, col_step) in enumerate([r[:2] for r in RIMS]):
        @pl.when(me.inside(row_step, col_step))
        def _():
            rim_copy(me, refs, sems, at).wait_send()


def lanes():
    return lax.broadcasted_iota(jnp.int32, (64, 128), 1)


def turn(v, by):
    by = by % 128
    return v if by == 0 else pltpu.roll(v, by, 1)


def gather_edges(rows, left, right, at):
    group = lanes() // 16
    low = turn(rows[0], 0)
    high = turn(rows[0], 16)
    for g in range(1, 8):
        low = jnp.where(group == g, turn(rows[g], 16 * g), low)
        high = jnp.where(group == g, turn(rows[g], 16 * (g + 1)), high)
    left[at] = low.astype(BF16)
    right[at] = high.astype(BF16)


def stack_taps(refs, stack):
    lane = lanes()

    def eight(at, carry):
        before = refs["from_left"][at].astype(F32)
        after = refs["from_right"][at].astype(F32)
        for g in range(8):
            e = at * 8 + g
            cells = refs["own"][e]
            c32 = cells.astype(F32)
            lower = jnp.where(lane < 16, turn(before, -16 * g), turn(c32, 16))
            upper = jnp.where(lane >= 112, turn(after, 112 - 16 * g), turn(c32, 112))
            stack[e, 0:64] = lower.astype(BF16)
            stack[e, 64:128] = cells
            stack[e, 128:192] = upper.astype(BF16)
        return carry

    lax.fori_loop(0, 12, eight, 0)


def window(stack, at):
    return jnp.concatenate(
        [
            jnp.concatenate([stack[at * 8 + r + 16 * a] for a in range(3)], axis=0)
            for r in range(8)
        ],
        axis=1,
    )


def rows_of(ref, at):
    return jnp.concatenate([ref[at * 8 + r] for r in range(8)], axis=1)


def strided(i):
    return pl.ds(i, 64, stride=64)


def block(n, at):
    return pl.ds(pl.multiple_of(n * 64 + at * 8, 8), 8)


def kernel(
    feat, cw, cb, wh, hb, dist, omega, mask,
    grad_out, cw_out, cb_out, wh_out, hb_out,
    flat, logit, held, own, left, right, from_left, from_right, stack, mixed,
    gown, gleft, gright, gfrom_left, gfrom_right, grads,
    wc, wf, whp, wht, bias_c, bias_h,
    packed, tmp, placed, sums, rows, src, parts, mine, whole, ring, dst,
    act_send, act_recv, grad_send, grad_recv,
    a_send, a_recv, b_send, b_recv,
    send_1, recv_1, send_2, recv_2, send_3, recv_3,
):
    me = Place()
    barrier = pltpu.get_barrier_semaphore()
    greet(me, barrier)
    act = dict(own=own, left=left, right=right, from_left=from_left, from_right=from_right)
    grd = dict(own=gown, left=gleft, right=gright, from_left=gfrom_left, from_right=gfrom_right)
    act_sems, grad_sems = (act_send, act_recv), (grad_send, grad_recv)

    def widen(c, carry):
        flat[pl.ds(pl.multiple_of(c * 64, 64), 64), :] = feat[c].astype(F32)
        return carry

    lax.fori_loop(0, 64, widen, 0)

    def activate(at, carry):
        rounded = []
        for g in range(8):
            i = at * 8 + g
            v = flat[strided(i), :]
            held[i] = v.astype(BF16)
            cells = jnp.where(v > 0.0, v, jnp.exp(jnp.minimum(v, 0.0)) - 1.0).astype(BF16)
            own[16 + i] = cells
            rounded.append(cells.astype(F32))
        gather_edges(rounded, left, right, at)
        return carry

    lax.fori_loop(0, 8, activate, 0)
    await_greetings(me, barrier)
    send_rims(me, act, act_sems)

    for k in range(9):
        wc[:, 64 * k : 64 * k + 64] = cw[k]
        wf[:, 64 * k : 64 * k + 64] = cw[8 - k].astype(F32).T.astype(BF16)
    whp[...] = jnp.zeros((64, 64), BF16)
    whp[0:NB, :] = wh[...]
    wht[...] = whp[...].astype(F32).T.astype(BF16)
    bias_c[...] = jnp.broadcast_to(cb[...], (128, 64)).T
    bias_h[...] = jnp.zeros((64, 128), F32)
    bias_h[0:NB, :] = jnp.broadcast_to(hb[...], (128, NB)).T

    await_rims(me, act, act_sems)
    stack_taps(act, stack)

    def forward(at, carry):
        pre = jnp.dot(wc[...], window(stack, at), preferred_element_type=F32)
        pre = pre + jnp.concatenate([bias_c[...]] * 8, axis=1)
        mix = (rows_of(held, at).astype(F32) + pre).astype(BF16)
        out = jnp.dot(whp[...], mix, preferred_element_type=F32)
        out = (out + jnp.concatenate([bias_h[...]] * 8, axis=1)).astype(BF16).astype(F32)
        for r in range(8):
            mixed[at * 8 + r] = mix[:, 128 * r : 128 * r + 128]
            logit[strided(at * 8 + r), :] = out[:, 128 * r : 128 * r + 128]
        return carry

    lax.fori_loop(0, 8, forward, 0)

    low = lanes() < 64

    def pack(m, carry):
        one = logit[pl.ds(pl.multiple_of(m * 64, 64), 64), :]
        two = logit[pl.ds(pl.multiple_of(m * 64 + 2048, 64), 64), :]
        packed[0, m] = jnp.where(low, one, turn(two, 64)).astype(BF16)
        packed[1, m] = jnp.where(low, turn(one, 64), two).astype(BF16)
        return carry

    lax.fori_loop(0, 32, pack, 0)

    def piece(k):
        return pl.ds(k * 2, 2)

    def mirror_a(t, carry):
        k = lax.rem(me.spot + t, 16)
        to = me.mirror_first(k)
        for h in range(2):
            @pl.when(me.is_me(to))
            def _():
                pltpu.make_async_copy(
                    packed.at[h, piece(k)], tmp.at[me.spot, h], a_recv.at[me.spot, h]
                ).start()

            @pl.when(jnp.logical_not(me.is_me(to)))
            def _():
                pltpu.make_async_remote_copy(
                    src_ref=packed.at[h, piece(k)], dst_ref=tmp.at[me.spot, h],
                    send_sem=a_send.at[k, h], recv_sem=a_recv.at[me.spot, h],
                    device_id=device(*to), device_id_type=MESH,
                ).start()
        return carry

    lax.fori_loop(0, 16, mirror_a, 0)

    def mirror_b(t, carry):
        s = lax.rem(me.spot + t, 16)
        for h in range(2):
            pltpu.make_async_copy(packed.at[h, piece(0)], tmp.at[s, h], a_recv.at[s, h]).wait()
            to = me.mirror_second(s, h)

            @pl.when(me.is_me(to))
            def _():
                pltpu.make_async_copy(
                    tmp.at[s, h], placed.at[me.core, piece(me.spot)], b_recv.at[me.core, me.spot]
                ).start()

            @pl.when(jnp.logical_not(me.is_me(to)))
            def _():
                pltpu.make_async_remote_copy(
                    src_ref=tmp.at[s, h], dst_ref=placed.at[me.core, piece(me.spot)],
                    send_sem=b_send.at[s, h], recv_sem=b_recv.at[me.core, me.spot],
                    device_id=device(*to), device_id_type=MESH,
                ).start()
        return carry

    lax.fori_loop(0, 16, mirror_b, 0)

    mine_first = mask[pl.ds(me.col // 2, 1), :].astype(F32)
    mine_first = jnp.broadcast_to(mine_first, (128, 128)).T
    first = jnp.where(me.core == 0, mine_first[0:64], mine_first[64:128])
    pair = first * mask[pl.ds(me.row, 1), :].astype(F32)
    count = jnp.sum(mask[...].astype(F32), keepdims=True)

    def arrive(k, carry):
        for c in range(2):
            pltpu.make_async_copy(
                tmp.at[0, 0], placed.at[c, piece(k)], b_recv.at[c, k]
            ).wait()
        for u in range(2):
            m = k * 2 + u
            other = jnp.concatenate([placed[0, m], placed[1, m]], axis=0).astype(F32).T
            one = pl.ds(pl.multiple_of(m * 64, 64), 64)
            two = pl.ds(pl.multiple_of(m * 64 + 2048, 64), 64)
            flat[one, :] = 0.5 * (logit[one, :] + other[0:64])
            flat[two, :] = 0.5 * (logit[two, :] + other[64:128])
        return carry

    lax.fori_loop(0, 16, arrive, 0)
    sums[0] = pair

    def softmaxes(at, carry):
        eight = pl.ds(pl.multiple_of(at * 8, 8), 8)
        weight = sums[0, eight, :]
        for start, stop, label in ((0, DB, dist), (DB, NB, omega)):
            chosen = label[eight, :]
            top = flat[block(start, at), :]
            for n in range(start + 1, stop):
                top = jnp.maximum(top, flat[block(n, at), :])
            below = jnp.zeros((8, 128), F32)
            for n in range(start, stop):
                e = jnp.exp(flat[block(n, at), :] - top)
                flat[block(n, at), :] = e
                below = below + e
            scale = 1.0 / below
            for n in range(start, stop):
                hot = jnp.where(chosen == n - start, 1.0, 0.0)
                flat[block(n, at), :] = weight * (flat[block(n, at), :] * scale - hot)
        for n in range(NB, 64):
            flat[block(n, at), :] = jnp.zeros((8, 128), F32)
        return carry

    lax.fori_loop(0, 8, softmaxes, 0)

    rows[...] = jnp.zeros((64, 640), F32)
    sums[...] = jnp.zeros((2, 64, 128), F32)

    def backward(at, carry):
        per_row = [flat[strided(at * 8 + r), :] for r in range(8)]
        bins = per_row[0]
        for r in range(1, 8):
            bins = bins + per_row[r]
        sums[0] += bins
        grad_logit = jnp.concatenate([v.astype(BF16) for v in per_row], axis=1)
        back = jnp.dot(wht[...], grad_logit, preferred_element_type=F32)
        pieces = [back[:, 128 * r : 128 * r + 128] for r in range(8)]
        total = pieces[0]
        for r in range(1, 8):
            total = total + pieces[r]
        sums[1] += total
        rounded = []
        for r in range(8):
            grads[at * 8 + r] = pieces[r]
            cells = pieces[r].astype(BF16)
            gown[16 + at * 8 + r] = cells
            rounded.append(cells.astype(F32))
        gather_edges(rounded, gleft, gright, at)
        over_pairs = (((1,), (1,)), ((), ()))
        rows[:, 0:576] += lax.dot_general(
            back.astype(BF16), window(stack, at), over_pairs, preferred_element_type=F32
        )
        rows[:, 576:640] += lax.dot_general(
            grad_logit, rows_of(mixed, at), over_pairs, preferred_element_type=F32
        )
        return carry

    lax.fori_loop(0, 8, backward, 0)
    send_rims(me, grd, grad_sems)

    rows[62:63, 576:640] = jnp.sum(sums[1].T, axis=0, keepdims=True)
    rows[63:64, 576:640] = jnp.sum(sums[0].T, axis=0, keepdims=True)
    for t in range(5):
        whole[64 * t : 64 * t + 64, :] = rows[:, 128 * t : 128 * t + 128]
    for s in range(32):
        src[s] = whole[10 * s : 10 * s + 10, :]
    slot = me.plane_slot()

    def send_parts(t, carry):
        s = lax.rem(slot + t, 32)
        pltpu.make_async_remote_copy(
            src_ref=src.at[s], dst_ref=parts.at[slot], send_sem=send_1.at[s],
            recv_sem=recv_1.at[slot], device_id=device(*me.plane(s)), device_id_type=MESH,
        ).start()
        return carry

    lax.fori_loop(1, 32, send_parts, 0)
    parts[slot] = src[slot]

    await_rims(me, grd, grad_sems)
    stack_taps(grd, stack)

    def wait_parts(t, carry):
        s = lax.rem(slot + t, 32)
        pltpu.make_async_copy(src.at[0], parts.at[s], recv_1.at[s]).wait()
        return carry

    lax.fori_loop(1, 32, wait_parts, 0)
    mine[0] = jnp.sum(parts[...], axis=0)
    ring[me.z] = mine[0]

    def send_ring(t, carry):
        o = lax.rem(me.z + t, 16)
        pltpu.make_async_remote_copy(
            src_ref=mine.at[0], dst_ref=ring.at[me.z], send_sem=send_2.at[o],
            recv_sem=recv_2.at[me.z], device_id=device(*me.ring(o)), device_id_type=MESH,
        ).start()
        return carry

    lax.fori_loop(1, 16, send_ring, 0)

    def inputs(at, carry):
        back = jnp.dot(wf[...], window(stack, at), preferred_element_type=F32)
        for r in range(8):
            i = at * 8 + r
            v = held[i].astype(F32)
            slope = jnp.where(v > 0.0, 1.0, jnp.exp(jnp.minimum(v, 0.0)))
            flat[strided(i), :] = grads[i] + slope * back[:, 128 * r : 128 * r + 128]
        return carry

    lax.fori_loop(0, 8, inputs, 0)

    def wait_ring(t, carry):
        o = lax.rem(me.z + t, 16)
        pltpu.make_async_copy(mine.at[0], ring.at[o], recv_2.at[o]).wait()
        return carry

    lax.fori_loop(1, 16, wait_ring, 0)
    mine[1] = jnp.sum(ring[...], axis=0)
    dst[slot] = mine[1]

    def send_all(t, carry):
        s = lax.rem(slot + t, 32)
        pltpu.make_async_remote_copy(
            src_ref=mine.at[1], dst_ref=dst.at[slot], send_sem=send_3.at[s],
            recv_sem=recv_3.at[slot], device_id=device(*me.plane(s)), device_id_type=MESH,
        ).start()
        return carry

    lax.fori_loop(1, 32, send_all, 0)

    def narrow(c, carry):
        grad_out[c] = flat[pl.ds(pl.multiple_of(c * 64, 64), 64), :].astype(BF16)
        return carry

    lax.fori_loop(0, 64, narrow, 0)

    def wait_all(t, carry):
        s = lax.rem(slot + t, 32)
        pltpu.make_async_copy(mine.at[1], dst.at[s], recv_3.at[s]).wait()
        return carry

    lax.fori_loop(1, 32, wait_all, 0)
    for s in range(32):
        whole[10 * s : 10 * s + 10, :] = dst[s]
    for k in range(9):
        t, half = k // 2, k % 2
        cw_out[k] = whole[64 * t : 64 * t + 64, 64 * half : 64 * half + 64] / count
    wh_out[...] = whole[256 : 256 + NB, 64:128] / count
    cb_out[...] = whole[318:319, 64:128] / count
    hb_out[...] = whole[319:320, 64 : 64 + NB] / count

    await_sent_rims(me, act, act_sems)
    await_sent_rims(me, grd, grad_sems)

    def sent_mirror(k, carry):
        for h in range(2):
            @pl.when(jnp.logical_not(me.is_me(me.mirror_first(k))))
            def _():
                pltpu.make_async_copy(packed.at[h, piece(k)], tmp.at[0, h], a_send.at[k, h]).wait()

            @pl.when(jnp.logical_not(me.is_me(me.mirror_second(k, h))))
            def _():
                pltpu.make_async_copy(tmp.at[k, h], placed.at[0, piece(0)], b_send.at[k, h]).wait()
        return carry

    lax.fori_loop(0, 16, sent_mirror, 0)

    def sent_plane(t, carry):
        s = lax.rem(slot + t, 32)
        pltpu.make_async_copy(mine.at[0], dst.at[s], send_1.at[s]).wait()
        pltpu.make_async_copy(mine.at[0], dst.at[s], send_3.at[s]).wait()
        return carry

    lax.fori_loop(1, 32, sent_plane, 0)

    def sent_ring(t, carry):
        o = lax.rem(me.z + t, 16)
        pltpu.make_async_copy(mine.at[0], ring.at[o], send_2.at[o]).wait()
        return carry

    lax.fori_loop(1, 16, sent_ring, 0)


def per_device(
    features, conv_weight, conv_bias, head_weight, head_bias, dist_label, omega_label, residue_mask
):
    vmem = pl.BlockSpec(memory_space=pltpu.VMEM)
    cells = (64, 128)
    dma = pltpu.SemaphoreType.DMA
    scratch = [
        pltpu.VMEM((4096, 128), F32),
        pltpu.VMEM((4096, 128), F32),
        pltpu.VMEM((64,) + cells, BF16),
        pltpu.VMEM((96,) + cells, BF16),
        pltpu.VMEM((8,) + cells, BF16),
        pltpu.VMEM((8,) + cells, BF16),
        pltpu.VMEM((12,) + cells, BF16),
        pltpu.VMEM((12,) + cells, BF16),
        pltpu.VMEM((96, 192, 128), BF16),
        pltpu.VMEM((64,) + cells, BF16),
        pltpu.VMEM((96,) + cells, BF16),
        pltpu.VMEM((8,) + cells, BF16),
        pltpu.VMEM((8,) + cells, BF16),
        pltpu.VMEM((12,) + cells, BF16),
        pltpu.VMEM((12,) + cells, BF16),
        pltpu.VMEM((64,) + cells, F32),
        pltpu.VMEM((64, 576), BF16),
        pltpu.VMEM((64, 576), BF16),
        pltpu.VMEM((64, 64), BF16),
        pltpu.VMEM((64, 64), BF16),
        pltpu.VMEM(cells, F32),
        pltpu.VMEM(cells, F32),
        pltpu.VMEM((2, 32) + cells, BF16),
        pltpu.VMEM((16, 2, 2) + cells, BF16),
        pltpu.VMEM((2, 32) + cells, BF16),
        pltpu.VMEM((2,) + cells, F32),
        pltpu.VMEM((64, 640), F32),
        pltpu.VMEM((32, 10, 128), F32),
        pltpu.VMEM((32, 10, 128), F32),
        pltpu.VMEM((2, 10, 128), F32),
        pltpu.VMEM((320, 128), F32),
        pltpu.VMEM((16, 10, 128), F32),
        pltpu.VMEM((32, 10, 128), F32),
        dma((8,)), dma((8,)), dma((8,)), dma((8,)),
        dma((16, 2)), dma((16, 2)), dma((16, 2)), dma((2, 16)),
        dma((32,)), dma((32,)), dma((16,)), dma((16,)), dma((32,)), dma((32,)),
    ]
    grad_input, conv_w, conv_b, head_w, head_b = pl.pallas_call(
        kernel,
        out_shape=(
            jax.ShapeDtypeStruct(features.shape, BF16),
            jax.ShapeDtypeStruct((9, 64, 64), F32),
            jax.ShapeDtypeStruct((1, 64), F32),
            jax.ShapeDtypeStruct((NB, 64), F32),
            jax.ShapeDtypeStruct((1, NB), F32),
        ),
        in_specs=[vmem] * 8,
        out_specs=(vmem,) * 5,
        scratch_shapes=scratch,
        compiler_params=pltpu.CompilerParams(collective_id=1, has_side_effects=True),
        name="pair_head",
    )(
        features,
        conv_weight.reshape(9, 64, 64),
        conv_bias.reshape(1, 64),
        head_weight,
        head_bias.reshape(1, NB),
        dist_label,
        omega_label,
        residue_mask.reshape(16, 128),
    )
    return (
        grad_input,
        conv_w.reshape(3, 3, 64, 64),
        conv_b.reshape(64),
        head_w,
        head_b.reshape(NB),
    )


def solution(mesh):
    return jax.shard_map(
        per_device,
        mesh=mesh,
        in_specs=(P(None, "col", "row"), P(), P(), P(), P(), P("col", "row"), P("col", "row"), P()),
        out_specs=(P(None, "col", "row"), P(), P(), P(), P()),
        check_vma=False,
    )
```

time: 910 us -> 180 us (0.20)
  waiting for transfers between devices: 481 us -> 0 us
  blocking collectives: 227 us -> 0 us
  Pallas kernels: 0 us -> 175 us
  local copies, waits for them, and re-layouts: 96.4 us -> 4.67 us
  starting transfers between devices: 31.4 us -> 0 us
  other arithmetic: 31.1 us -> 0 us
  matrix products: 23.1 us -> 0 us
  between operations: 14.9 us -> 0.66 us
    psum x1 -> x0, waiting for transfers between devices: 450 us -> none  [per_device(): lax.psum((conv_w_term, conv_b_term, head_w_term, head_b_term), ('row', 'c...]
    pallas_call x0 -> x1, Pallas kernels: none -> 175 us  [per_device(): pl.pallas_call(kernel, out_shape=(jax.ShapeDtypeStruct(features.shape, BF...]
    all_to_all x2 -> x0, blocking collectives: 127 us -> none  [the longest x1 90.6 us: mirror(): lax.all_to_all(lax.all_to_all(sectioned, 'col', split_axis=3, concat_axis...]
    psum x1 -> x0, blocking collectives: 100 us -> none  [per_device(): lax.psum((conv_w_term, conv_b_term, head_w_term, head_b_term), ('row', 'c...]
    unnamed x62 -> x13, local copies, waits for them, and re-layouts: 34.1 us -> 4.67 us
    ppermute x8 -> x0, starting transfers between devices: 25 us -> none  [the longest x4 15.1 us: with_halo(): lax.ppermute(tail, axis, [(i, (i + 1) % count) for i in range(ends)])]
    all_to_all x1 -> x0, waiting for transfers between devices: 24.9 us -> none  [mirror(): lax.all_to_all(ordered, 'col', split_axis=1, concat_axis=3, tiled=True)]
    dot_general x12 -> x0, matrix products: 23.1 us -> none  [the longest x6 14.5 us: dilated(): jnp.einsum('ok,kxy->oxy', tap_matrix(weight, first_member), stacked, pref...]
  transfers between devices with their start and end apart: 10 -> 0, of which waited for: 5 -> 0; matrix products, arithmetic and copies ran while one was open for 3% -> 0% of each run, Pallas kernels for 0% -> 0%
where the time goes in v2:
time: 180 us
  Pallas kernels  175 us (97%)
  local copies, waits for them, and re-layouts  4.67 us (3%)
    pallas_call x1, Pallas kernels, per_device(): pl.pallas_call(kernel, out_shape=(jax.ShapeDtypeStruct(features.shape, BF...  175 us
    unnamed x13, local copies, waits for them, and re-layouts  4.67 us

profile of v2, /device:TPU:1, one launch (start us, length us, event | category | flops | bytes accessed | tf_op | source)
XLA Modules:
  0.0 180.0 jit_solution(16552562128208781140)
XLA Ops:
  0.6 174.6 %pair_head.1 = (bf16[64,64,128]{2,1,0:T(8,128)(2,1)}, f32[9,64,64]{2,1,0:T(8,128)}, f32[1,64]{1,0:T(1,128)}, f32[62,64]{1,0:T(8,128)}, f32[1,62]{1,0:T(1,128)}) custom-call(bf16[64,64,128]{2,1,0:T(8,128)(2,1)} %feat.1, bf16[9,64,64]{2,1,0:T(8,128)(2,1)} %bitcast.8, f32[1,64]{1,0:T(1,128)} %bitcast.10, bf16[62,64]{1,0:T(8,128)(2,1)} %wh.1, f32[1,62]{1,0:T(1,128)} %bitcast.11, ...), custom_call_target="tpu_custom_call" | custom-call | tf_op jit(solution)/shard_map/pair_head/pallas_call | solution.py:580
  175.3 0.0 copy-start
  175.3 2.3 %copy.18 = bf16[64,64,128]{2,1,0:T(8,128)(2,1)} copy(bf16[64,64,128]{2,1,0:T(8,128)(2,1)} %get-tuple-element.20) | data formatting | bytes 2097152
  177.6 0.0 copy-done
  177.6 0.0 copy-start.3
  177.6 0.0 copy-start.1
  177.6 0.7 copy.19
  178.3 0.0 copy-done.3
  178.3 0.5 copy.20
  178.8 0.0 copy-done.1
  178.8 0.0 copy-start.2
  178.8 0.6 copy.21
  179.5 0.0 copy-done.2
  179.5 0.5 copy.22
Async XLA Ops:
  175.3 2.3 %copy-start = (f32[9,64,64]{2,1,0:T(8,128)S(1)}, f32[9,64,64]{2,1,0:T(8,128)}, u32[]{:S(2)}) copy-start(f32[9,64,64]{2,1,0:T(8,128)} %get-tuple-element.11) | copy-start | bytes 442372
  177.6 0.7 copy-start.3
  177.6 1.2 copy-start.1
  178.8 0.6 copy-start.2

commit v3 on v2

--- a/solution.py
+++ b/solution.py
@@ -12,18 +12,10 @@
 BF16 = jnp.bfloat16
 DB = 37
 NB = 62
-
-RIMS = (
-    (0, 1, "own", 64, 16, "own", 0),
-    (0, -1, "own", 16, 16, "own", 80),
-    (1, 0, "right", 0, 8, "from_left", 2),
-    (-1, 0, "left", 0, 8, "from_right", 2),
-    (1, 1, "right", 6, 2, "from_left", 0),
-    (1, -1, "right", 0, 2, "from_left", 10),
-    (-1, 1, "left", 6, 2, "from_right", 0),
-    (-1, -1, "left", 0, 2, "from_right", 10),
+RIM_SEMS = (
+    "band_send", "band_recv", "edge_send", "edge_recv", "via_send", "via_recv",
+    "relay_send", "corner_send", "corner_recv",
 )
-
 
 def device(x, y, z, core):
     return ((z // 4) * 4 + x, (y * 4 + lax.rem(z, 4)) * 2 + core)
@@ -37,12 +29,9 @@
         self.core = lax.rem(self.col, 2)
         chip = self.col // 2
         self.y = chip // 4
-        self.z = 4 * (self.row // 4) + lax.rem(chip, 4)
+        self.block = self.row // 4
+        self.z = 4 * self.block + lax.rem(chip, 4)
         self.spot = 4 * self.y + self.x
-
-    def inside(self, row_step, col_step):
-        row, col = self.row + row_step, self.col + col_step
-        return (row >= 0) & (row < 16) & (col >= 0) & (col < 32)
 
     def is_me(self, t):
         return (t[0] == self.x) & (t[1] == self.y) & (t[2] == self.z) & (t[3] == self.core)
@@ -70,11 +59,62 @@
     pl.semaphore_signal(barrier, inc=1, device_id=target, device_id_type=MESH)
 
 
+def next_along_row(me, flow):
+    return (me.row + 1, me.col) if flow == 0 else (me.row - 1, me.col)
+
+
+def near(me, flow):
+    return me.x < 3 if flow == 0 else me.x > 0
+
+
+def far_open(me, flow):
+    return me.block < 3 if flow == 0 else me.block > 0
+
+
+def far_source(flow):
+    return 3 if flow == 0 else 0
+
+
+def far_target(me, flow):
+    if flow == 0:
+        return device(0, me.y, me.z + 4, me.core)
+    return device(3, me.y, me.z - 4, me.core)
+
+
+def receives(me, flow):
+    return me.row > 0 if flow == 0 else me.row < 15
+
+
+def col_open(me, side):
+    return me.col > 0 if side == 0 else me.col < 31
+
+
+def next_along_col(me, side):
+    return (me.row, me.col - 1) if side == 0 else (me.row, me.col + 1)
+
+
 def greet(me, barrier):
-    for row_step, col_step in [r[:2] for r in RIMS]:
-        @pl.when(me.inside(row_step, col_step))
-        def _():
-            signal(barrier, (me.row + row_step, me.col + col_step))
+    for side in range(2):
+        @pl.when(col_open(me, side))
+        def _():
+            signal(barrier, next_along_col(me, side))
+
+    for flow in range(2):
+        @pl.when(near(me, flow))
+        def _():
+            signal(barrier, next_along_row(me, flow))
+
+    def far_partners(k, carry):
+        @pl.when((me.x == 0) & (me.block > 0))
+        def _():
+            signal(barrier, device(k, me.y, me.z - 4, me.core))
+
+        @pl.when((me.x == 3) & (me.block < 3))
+        def _():
+            signal(barrier, device(k, me.y, me.z + 4, me.core))
+        return carry
+
+    lax.fori_loop(0, 4, far_partners, 0)
 
     def mirror_partners(s, carry):
         for t in (me.mirror_first(s), me.mirror_giver(s, 0), me.mirror_giver(s, 1)):
@@ -99,47 +139,165 @@
 
 
 def await_greetings(me, barrier):
-    rows = 3 - jnp.where(me.row == 0, 1, 0) - jnp.where(me.row == 15, 1, 0)
-    cols = 3 - jnp.where(me.col == 0, 1, 0) - jnp.where(me.col == 31, 1, 0)
-    others = 46 + 47 - jnp.where(me.spot == me.z, 1, 0)
-    pl.semaphore_wait(barrier, rows * cols - 1 + others)
-
-
-def rim_copy(me, refs, sems, at):
-    row_step, col_step, source, first, many, target, into = RIMS[at]
+    total = 46 + 47 - jnp.where(me.spot == me.z, 1, 0)
+    for k in range(2):
+        for known in (col_open(me, k), near(me, k), far_open(me, k)):
+            total = total + jnp.where(known, 1, 0)
+    pl.semaphore_wait(barrier, total)
+
+
+def remote(source, target, sent, arrived, to):
     return pltpu.make_async_remote_copy(
-        src_ref=refs[source].at[pl.ds(first, many)],
-        dst_ref=refs[target].at[pl.ds(into, many)],
-        send_sem=sems[0].at[at],
-        recv_sem=sems[1].at[at],
-        device_id=(me.row + row_step, me.col + col_step),
-        device_id_type=MESH,
+        src_ref=source, dst_ref=target, send_sem=sent, recv_sem=arrived,
+        device_id=to, device_id_type=MESH,
+    )
+
+
+def edge(refs, flow, k):
+    return refs[("right", "left")[flow]].at[pl.ds(2 * k, 2)]
+
+
+def rim(refs, flow, k):
+    return refs[("from_left", "from_right")[flow]].at[pl.ds(2 * k + 2, 2)]
+
+
+def band_copy(me, refs, sems, side):
+    first, into = ((16, 80), (64, 0))[side]
+    return remote(
+        refs["own"].at[pl.ds(first, 16)], refs["own"].at[pl.ds(into, 16)],
+        sems["band_send"].at[side], sems["band_recv"].at[side], next_along_col(me, side),
+    )
+
+
+def edge_copy(me, refs, sems, flow, k, to):
+    return remote(
+        edge(refs, flow, k), rim(refs, flow, k),
+        sems["edge_send"].at[flow, k], sems["edge_recv"].at[flow, k], to,
+    )
+
+
+def via_copy(me, refs, sems, flow, k):
+    return remote(
+        edge(refs, flow, k), refs["via"].at[flow],
+        sems["via_send"].at[flow, k], sems["via_recv"].at[flow],
+        device(k, me.y, me.z, me.core),
+    )
+
+
+def relay_copy(me, refs, sems, flow):
+    return remote(
+        refs["via"].at[flow], rim(refs, flow, me.x),
+        sems["relay_send"].at[flow], sems["edge_recv"].at[flow, me.x], far_target(me, flow),
+    )
+
+
+def corner_copy(me, refs, sems, flow, side):
+    held = refs[("from_left", "from_right")[flow]]
+    first, into = ((2, 10), (8, 0))[side]
+    return remote(
+        held.at[pl.ds(first, 2)], held.at[pl.ds(into, 2)],
+        sems["corner_send"].at[flow, side], sems["corner_recv"].at[flow, side],
+        next_along_col(me, side),
     )
 
 
 def send_rims(me, refs, sems):
-    for at, (row_step, col_step, _, _, many, target, into) in enumerate(RIMS):
-        @pl.when(me.inside(row_step, col_step))
-        def _():
-            rim_copy(me, refs, sems, at).start()
-
-        @pl.when(jnp.logical_not(me.inside(-row_step, -col_step)))
-        def _():
-            refs[target][into : into + many] = jnp.zeros((many, 64, 128), BF16)
+    for flow in range(2):
+        own = far_source(flow)
+
+        @pl.when((me.x == own) & far_open(me, flow))
+        def _():
+            for k in range(4):
+                if k != own:
+                    via_copy(me, refs, sems, flow, k).start()
+            edge_copy(me, refs, sems, flow, own, far_target(me, flow)).start()
+
+        @pl.when(near(me, flow))
+        def _():
+            for k in range(4):
+                edge_copy(me, refs, sems, flow, k, next_along_row(me, flow)).start()
+
+    for side in range(2):
+        @pl.when(col_open(me, side))
+        def _():
+            band_copy(me, refs, sems, side).start()
+
+        @pl.when(jnp.logical_not(col_open(me, side)))
+        def _():
+            into = (0, 80)[side]
+            refs["own"][into : into + 16] = jnp.zeros((16, 64, 128), BF16)
+            into = (0, 10)[side]
+            refs["from_left"][into : into + 2] = jnp.zeros((2, 64, 128), BF16)
+            refs["from_right"][into : into + 2] = jnp.zeros((2, 64, 128), BF16)
+
+    for flow in range(2):
+        @pl.when(jnp.logical_not(receives(me, flow)))
+        def _():
+            refs[("from_left", "from_right")[flow]][...] = jnp.zeros((12, 64, 128), BF16)
+
+
+def relay_rims(me, refs, sems):
+    for flow in range(2):
+        @pl.when((me.x != far_source(flow)) & far_open(me, flow))
+        def _():
+            via_copy(me, refs, sems, flow, 0).wait_recv()
+            relay_copy(me, refs, sems, flow).start()
 
 
 def await_rims(me, refs, sems):
-    for at, (row_step, col_step) in enumerate([r[:2] for r in RIMS]):
-        @pl.when(me.inside(-row_step, -col_step))
-        def _():
-            rim_copy(me, refs, sems, at).wait_recv()
+    for flow in range(2):
+        for k in (0, 3, 1, 2):
+            @pl.when(receives(me, flow))
+            def _():
+                edge_copy(me, refs, sems, flow, k, next_along_row(me, flow)).wait_recv()
+
+            if k in (0, 3):
+                side = k // 3
+
+                @pl.when(receives(me, flow) & col_open(me, side))
+                def _():
+                    corner_copy(me, refs, sems, flow, side).start()
+
+    for side in range(2):
+        @pl.when(col_open(me, 1 - side))
+        def _():
+            band_copy(me, refs, sems, side).wait_recv()
+
+        for flow in range(2):
+            @pl.when(receives(me, flow) & col_open(me, 1 - side))
+            def _():
+                corner_copy(me, refs, sems, flow, side).wait_recv()
 
 
 def await_sent_rims(me, refs, sems):
-    for at, (row_step, col_step) in enumerate([r[:2] for r in RIMS]):
-        @pl.when(me.inside(row_step, col_step))
-        def _():
-            rim_copy(me, refs, sems, at).wait_send()
+    for flow in range(2):
+        own = far_source(flow)
+
+        @pl.when((me.x == own) & far_open(me, flow))
+        def _():
+            for k in range(4):
+                if k != own:
+                    via_copy(me, refs, sems, flow, k).wait_send()
+            edge_copy(me, refs, sems, flow, own, far_target(me, flow)).wait_send()
+
+        @pl.when((me.x != own) & far_open(me, flow))
+        def _():
+            relay_copy(me, refs, sems, flow).wait_send()
+
+        @pl.when(near(me, flow))
+        def _():
+            for k in range(4):
+                edge_copy(me, refs, sems, flow, k, next_along_row(me, flow)).wait_send()
+
+        for side in range(2):
+            @pl.when(receives(me, flow) & col_open(me, side))
+            def _():
+                corner_copy(me, refs, sems, flow, side).wait_send()
+
+    for side in range(2):
+        @pl.when(col_open(me, side))
+        def _():
+            band_copy(me, refs, sems, side).wait_send()
 
 
 def lanes():
@@ -207,20 +365,21 @@
 def kernel(
     feat, cw, cb, wh, hb, dist, omega, mask,
     grad_out, cw_out, cb_out, wh_out, hb_out,
-    flat, logit, held, own, left, right, from_left, from_right, stack, mixed,
-    gown, gleft, gright, gfrom_left, gfrom_right, grads,
+    flat, logit, held, own, left, right, from_left, from_right, via, stack, mixed,
+    gown, gleft, gright, gfrom_left, gfrom_right, gvia, grads,
     wc, wf, whp, wht, bias_c, bias_h,
     packed, tmp, placed, sums, rows, src, parts, mine, whole, ring, dst,
-    act_send, act_recv, grad_send, grad_recv,
     a_send, a_recv, b_send, b_recv,
     send_1, recv_1, send_2, recv_2, send_3, recv_3,
+    *rim_sems,
 ):
+    act_sems = dict(zip(RIM_SEMS, rim_sems[:9]))
+    grad_sems = dict(zip(RIM_SEMS, rim_sems[9:]))
     me = Place()
     barrier = pltpu.get_barrier_semaphore()
     greet(me, barrier)
-    act = dict(own=own, left=left, right=right, from_left=from_left, from_right=from_right)
-    grd = dict(own=gown, left=gleft, right=gright, from_left=gfrom_left, from_right=gfrom_right)
-    act_sems, grad_sems = (act_send, act_recv), (grad_send, grad_recv)
+    act = dict(own=own, left=left, right=right, from_left=from_left, from_right=from_right, via=via)
+    grd = dict(own=gown, left=gleft, right=gright, from_left=gfrom_left, from_right=gfrom_right, via=gvia)
 
     def widen(c, carry):
         flat[pl.ds(pl.multiple_of(c * 64, 64), 64), :] = feat[c].astype(F32)
@@ -244,6 +403,8 @@
     await_greetings(me, barrier)
     send_rims(me, act, act_sems)
 
+    relay_rims(me, act, act_sems)
+
     for k in range(9):
         wc[:, 64 * k : 64 * k + 64] = cw[k]
         wf[:, 64 * k : 64 * k + 64] = cw[8 - k].astype(F32).T.astype(BF16)
@@ -284,8 +445,11 @@
     def piece(k):
         return pl.ds(k * 2, 2)
 
+    apart = lax.rem(me.spot - me.z + 16, 16)
+    apart = lax.rem(jnp.minimum(apart, 16 - apart), 8)
+
     def mirror_a(t, carry):
-        k = lax.rem(me.spot + t, 16)
+        k = lax.rem(apart - t // 2 + 8, 8) + 8 * lax.rem(t, 2)
         to = me.mirror_first(k)
         for h in range(2):
             @pl.when(me.is_me(to))
@@ -306,7 +470,9 @@
     lax.fori_loop(0, 16, mirror_a, 0)
 
     def mirror_b(t, carry):
-        s = lax.rem(me.spot + t, 16)
+        p = lax.rem(me.spot + t // 2, 8)
+        back = jnp.where(p == 0, 8, 16 - p)
+        s = lax.rem(me.z + jnp.where(lax.rem(t, 2) == 0, p, back), 16)
         for h in range(2):
             pltpu.make_async_copy(packed.at[h, piece(0)], tmp.at[s, h], a_recv.at[s, h]).wait()
             to = me.mirror_second(s, h)
@@ -428,8 +594,7 @@
     lax.fori_loop(1, 32, send_parts, 0)
     parts[slot] = src[slot]
 
-    await_rims(me, grd, grad_sems)
-    stack_taps(grd, stack)
+    relay_rims(me, grd, grad_sems)
 
     def wait_parts(t, carry):
         s = lax.rem(slot + t, 32)
@@ -449,6 +614,9 @@
         return carry
 
     lax.fori_loop(1, 16, send_ring, 0)
+
+    await_rims(me, grd, grad_sems)
+    stack_taps(grd, stack)
 
     def inputs(at, carry):
         back = jnp.dot(wf[...], window(stack, at), preferred_element_type=F32)
@@ -548,6 +716,7 @@
         pltpu.VMEM((8,) + cells, BF16),
         pltpu.VMEM((12,) + cells, BF16),
         pltpu.VMEM((12,) + cells, BF16),
+        pltpu.VMEM((2, 2) + cells, BF16),
         pltpu.VMEM((96, 192, 128), BF16),
         pltpu.VMEM((64,) + cells, BF16),
         pltpu.VMEM((96,) + cells, BF16),
@@ -555,6 +724,7 @@
         pltpu.VMEM((8,) + cells, BF16),
         pltpu.VMEM((12,) + cells, BF16),
         pltpu.VMEM((12,) + cells, BF16),
+        pltpu.VMEM((2, 2) + cells, BF16),
         pltpu.VMEM((64,) + cells, F32),
         pltpu.VMEM((64, 576), BF16),
         pltpu.VMEM((64, 576), BF16),
@@ -573,9 +743,11 @@
         pltpu.VMEM((320, 128), F32),
         pltpu.VMEM((16, 10, 128), F32),
         pltpu.VMEM((32, 10, 128), F32),
-        dma((8,)), dma((8,)), dma((8,)), dma((8,)),
         dma((16, 2)), dma((16, 2)), dma((16, 2)), dma((2, 16)),
         dma((32,)), dma((32,)), dma((16,)), dma((16,)), dma((32,)), dma((32,)),
+    ] + 2 * [
+        dma((2,)), dma((2,)), dma((2, 4)), dma((2, 4)), dma((2, 4)), dma((2,)),
+        dma((2,)), dma((2, 2)), dma((2, 2)),
     ]
     grad_input, conv_w, conv_b, head_w, head_b = pl.pallas_call(
         kernel,

time: 180 us -> 149 us (0.83)
  Pallas kernels: 175 us -> 143 us
    pallas_call x1, Pallas kernels: 175 us -> 143 us  [per_device(): pl.pallas_call(kernel, out_shape=(jax.ShapeDtypeStruct(features.shape, BF...]
where the time goes in v3:
time: 149 us
  Pallas kernels  143 us (96%)
  local copies, waits for them, and re-layouts  4.67 us (3%)
    pallas_call x1, Pallas kernels, per_device(): pl.pallas_call(kernel, out_shape=(jax.ShapeDtypeStruct(features.shape, BF...  143 us
    unnamed x13, local copies, waits for them, and re-layouts  4.67 us

profile of v3, /device:TPU:1, one launch (start us, length us, event | category | flops | bytes accessed | tf_op | source)
XLA Modules:
  0.0 148.6 jit_solution(13996023725496869225)
XLA Ops:
  0.6 143.3 %pair_head.1 = (bf16[64,64,128]{2,1,0:T(8,128)(2,1)}, f32[9,64,64]{2,1,0:T(8,128)}, f32[1,64]{1,0:T(1,128)}, f32[62,64]{1,0:T(8,128)}, f32[1,62]{1,0:T(1,128)}) custom-call(bf16[64,64,128]{2,1,0:T(8,128)(2,1)} %feat.1, bf16[9,64,64]{2,1,0:T(8,128)(2,1)} %bitcast.8, f32[1,64]{1,0:T(1,128)} %bitcast.10, bf16[62,64]{1,0:T(8,128)(2,1)} %wh.1, f32[1,62]{1,0:T(1,128)} %bitcast.11, ...), custom_call_target="tpu_custom_call" | custom-call | tf_op jit(solution)/shard_map/pair_head/pallas_call | solution.py:752
  143.9 0.0 copy-start
  143.9 2.3 %copy.18 = bf16[64,64,128]{2,1,0:T(8,128)(2,1)} copy(bf16[64,64,128]{2,1,0:T(8,128)(2,1)} %get-tuple-element.20) | data formatting | bytes 2097152
  146.3 0.0 copy-done
  146.3 0.0 copy-start.3
  146.3 0.0 copy-start.1
  146.3 0.7 copy.19
  147.0 0.0 copy-done.3
  147.0 0.5 copy.20
  147.5 0.0 copy-done.1
  147.5 0.0 copy-start.2
  147.5 0.6 copy.21
  148.1 0.0 copy-done.2
  148.1 0.5 copy.22
Async XLA Ops:
  143.9 2.3 %copy-start = (f32[9,64,64]{2,1,0:T(8,128)S(1)}, f32[9,64,64]{2,1,0:T(8,128)}, u32[]{:S(2)}) copy-start(f32[9,64,64]{2,1,0:T(8,128)} %get-tuple-element.11) | copy-start | bytes 442372
  146.3 0.7 copy-start.3
  146.3 1.2 copy-start.1
  147.5 0.6 copy-start.2

commit v4 on v3

--- a/solution.py
+++ b/solution.py
@@ -320,7 +320,7 @@
     right[at] = high.astype(BF16)
 
 
-def stack_taps(refs, stack):
+def stack_taps(refs, stack, first, last):
     lane = lanes()
 
     def eight(at, carry):
@@ -337,7 +337,7 @@
             stack[e, 128:192] = upper.astype(BF16)
         return carry
 
-    lax.fori_loop(0, 12, eight, 0)
+    lax.fori_loop(first, last, eight, 0)
 
 
 def window(stack, at):
@@ -364,9 +364,9 @@
 
 def kernel(
     feat, cw, cb, wh, hb, dist, omega, mask,
-    grad_out, cw_out, cb_out, wh_out, hb_out,
+    grad_out, sums_out,
     flat, logit, held, own, left, right, from_left, from_right, via, stack, mixed,
-    gown, gleft, gright, gfrom_left, gfrom_right, gvia, grads,
+    gown, gleft, gright, gfrom_left, gfrom_right, gvia, grads, glogit,
     wc, wf, whp, wht, bias_c, bias_h,
     packed, tmp, placed, sums, rows, src, parts, mine, whole, ring, dst,
     a_send, a_recv, b_send, b_recv,
@@ -416,7 +416,6 @@
     bias_h[0:NB, :] = jnp.broadcast_to(hb[...], (128, NB)).T
 
     await_rims(me, act, act_sems)
-    stack_taps(act, stack)
 
     def forward(at, carry):
         pre = jnp.dot(wc[...], window(stack, at), preferred_element_type=F32)
@@ -429,82 +428,108 @@
             logit[strided(at * 8 + r), :] = out[:, 128 * r : 128 * r + 128]
         return carry
 
-    lax.fori_loop(0, 8, forward, 0)
-
-    low = lanes() < 64
-
-    def pack(m, carry):
-        one = logit[pl.ds(pl.multiple_of(m * 64, 64), 64), :]
-        two = logit[pl.ds(pl.multiple_of(m * 64 + 2048, 64), 64), :]
-        packed[0, m] = jnp.where(low, one, turn(two, 64)).astype(BF16)
-        packed[1, m] = jnp.where(low, turn(one, 64), two).astype(BF16)
-        return carry
-
-    lax.fori_loop(0, 32, pack, 0)
-
-    def piece(k):
-        return pl.ds(k * 2, 2)
+    def pack(part):
+        low = lax.broadcasted_iota(jnp.int32, (32, 128), 1) < 64
+        at = 32 * part
+
+        def step(m, carry):
+            one = logit[pl.ds(pl.multiple_of(m * 64 + at, 32), 32), :]
+            two = logit[pl.ds(pl.multiple_of(m * 64 + 2048 + at, 32), 32), :]
+            packed[0, m, at : at + 32] = jnp.where(low, one, turn(two, 64)).astype(BF16)
+            packed[1, m, at : at + 32] = jnp.where(low, turn(one, 64), two).astype(BF16)
+            return carry
+
+        lax.fori_loop(0, 32, step, 0)
+
+    def piece(ref, h, k, part):
+        return ref.at[h, pl.ds(k * 2, 2), pl.ds(32 * part, 32)]
 
     apart = lax.rem(me.spot - me.z + 16, 16)
     apart = lax.rem(jnp.minimum(apart, 16 - apart), 8)
 
-    def mirror_a(t, carry):
-        k = lax.rem(apart - t // 2 + 8, 8) + 8 * lax.rem(t, 2)
-        to = me.mirror_first(k)
-        for h in range(2):
-            @pl.when(me.is_me(to))
-            def _():
-                pltpu.make_async_copy(
-                    packed.at[h, piece(k)], tmp.at[me.spot, h], a_recv.at[me.spot, h]
-                ).start()
-
-            @pl.when(jnp.logical_not(me.is_me(to)))
-            def _():
-                pltpu.make_async_remote_copy(
-                    src_ref=packed.at[h, piece(k)], dst_ref=tmp.at[me.spot, h],
-                    send_sem=a_send.at[k, h], recv_sem=a_recv.at[me.spot, h],
-                    device_id=device(*to), device_id_type=MESH,
-                ).start()
-        return carry
-
-    lax.fori_loop(0, 16, mirror_a, 0)
-
-    def mirror_b(t, carry):
+    def mirror_a(part):
+        def step(t, carry):
+            k = lax.rem(apart - t // 2 + 8, 8) + 8 * lax.rem(t, 2)
+            to = me.mirror_first(k)
+            for h in range(2):
+                @pl.when(me.is_me(to))
+                def _():
+                    pltpu.make_async_copy(
+                        piece(packed, h, k, part), tmp.at[part, me.spot, h],
+                        a_recv.at[part, me.spot, h],
+                    ).start()
+
+                @pl.when(jnp.logical_not(me.is_me(to)))
+                def _():
+                    remote(
+                        piece(packed, h, k, part), tmp.at[part, me.spot, h],
+                        a_send.at[part, k, h], a_recv.at[part, me.spot, h], device(*to),
+                    ).start()
+            return carry
+
+        lax.fori_loop(0, 16, step, 0)
+
+    def mirror_b(part, t):
         p = lax.rem(me.spot + t // 2, 8)
         back = jnp.where(p == 0, 8, 16 - p)
         s = lax.rem(me.z + jnp.where(lax.rem(t, 2) == 0, p, back), 16)
         for h in range(2):
-            pltpu.make_async_copy(packed.at[h, piece(0)], tmp.at[s, h], a_recv.at[s, h]).wait()
+            pltpu.make_async_copy(
+                piece(packed, h, 0, part), tmp.at[part, s, h], a_recv.at[part, s, h]
+            ).wait()
             to = me.mirror_second(s, h)
 
             @pl.when(me.is_me(to))
             def _():
                 pltpu.make_async_copy(
-                    tmp.at[s, h], placed.at[me.core, piece(me.spot)], b_recv.at[me.core, me.spot]
+                    tmp.at[part, s, h], piece(placed, me.core, me.spot, part),
+                    b_recv.at[part, me.core, me.spot],
                 ).start()
 
             @pl.when(jnp.logical_not(me.is_me(to)))
             def _():
-                pltpu.make_async_remote_copy(
-                    src_ref=tmp.at[s, h], dst_ref=placed.at[me.core, piece(me.spot)],
-                    send_sem=b_send.at[s, h], recv_sem=b_recv.at[me.core, me.spot],
-                    device_id=device(*to), device_id_type=MESH,
+                remote(
+                    tmp.at[part, s, h], piece(placed, me.core, me.spot, part),
+                    b_send.at[part, s, h], b_recv.at[part, me.core, me.spot], device(*to),
                 ).start()
-        return carry
-
-    lax.fori_loop(0, 16, mirror_b, 0)
+
+    stack_taps(act, stack, 0, 8)
+    lax.fori_loop(0, 4, forward, 0)
+    pack(0)
+    mirror_a(0)
+    stack_taps(act, stack, 8, 12)
+
+    def forward_and_pass(at, carry):
+        forward(at, carry)
+
+        def pass_on(u, inner):
+            mirror_b(0, (at - 4) * 4 + u)
+            return inner
+
+        lax.fori_loop(0, 4, pass_on, 0)
+        return carry
+
+    lax.fori_loop(4, 8, forward_and_pass, 0)
+    pack(1)
+    mirror_a(1)
+
+    def pass_rest(t, carry):
+        mirror_b(1, t)
+        return carry
+
+    lax.fori_loop(0, 16, pass_rest, 0)
 
     mine_first = mask[pl.ds(me.col // 2, 1), :].astype(F32)
     mine_first = jnp.broadcast_to(mine_first, (128, 128)).T
     first = jnp.where(me.core == 0, mine_first[0:64], mine_first[64:128])
     pair = first * mask[pl.ds(me.row, 1), :].astype(F32)
-    count = jnp.sum(mask[...].astype(F32), keepdims=True)
 
     def arrive(k, carry):
         for c in range(2):
-            pltpu.make_async_copy(
-                tmp.at[0, 0], placed.at[c, piece(k)], b_recv.at[c, k]
-            ).wait()
+            for part in range(2):
+                pltpu.make_async_copy(
+                    tmp.at[part, 0, 0], piece(placed, c, k, part), b_recv.at[part, c, k]
+                ).wait()
         for u in range(2):
             m = k * 2 + u
             other = jnp.concatenate([placed[0, m], placed[1, m]], axis=0).astype(F32).T
@@ -549,6 +574,8 @@
         for r in range(1, 8):
             bins = bins + per_row[r]
         sums[0] += bins
+        for r in range(8):
+            glogit[at * 8 + r] = per_row[r].astype(BF16)
         grad_logit = jnp.concatenate([v.astype(BF16) for v in per_row], axis=1)
         back = jnp.dot(wht[...], grad_logit, preferred_element_type=F32)
         pieces = [back[:, 128 * r : 128 * r + 128] for r in range(8)]
@@ -563,17 +590,24 @@
             gown[16 + at * 8 + r] = cells
             rounded.append(cells.astype(F32))
         gather_edges(rounded, gleft, gright, at)
+        return carry
+
+    lax.fori_loop(0, 8, backward, 0)
+    send_rims(me, grd, grad_sems)
+
+    def weights(at, carry):
         over_pairs = (((1,), (1,)), ((), ()))
         rows[:, 0:576] += lax.dot_general(
-            back.astype(BF16), window(stack, at), over_pairs, preferred_element_type=F32
+            jnp.concatenate([gown[16 + at * 8 + r] for r in range(8)], axis=1),
+            window(stack, at), over_pairs, preferred_element_type=F32,
         )
         rows[:, 576:640] += lax.dot_general(
-            grad_logit, rows_of(mixed, at), over_pairs, preferred_element_type=F32
+            rows_of(glogit, at), rows_of(mixed, at), over_pairs, preferred_element_type=F32
         )
         return carry
 
-    lax.fori_loop(0, 8, backward, 0)
-    send_rims(me, grd, grad_sems)
+    lax.fori_loop(0, 8, weights, 0)
+    relay_rims(me, grd, grad_sems)
 
     rows[62:63, 576:640] = jnp.sum(sums[1].T, axis=0, keepdims=True)
     rows[63:64, 576:640] = jnp.sum(sums[0].T, axis=0, keepdims=True)
@@ -594,8 +628,6 @@
     lax.fori_loop(1, 32, send_parts, 0)
     parts[slot] = src[slot]
 
-    relay_rims(me, grd, grad_sems)
-
     def wait_parts(t, carry):
         s = lax.rem(slot + t, 32)
         pltpu.make_async_copy(src.at[0], parts.at[s], recv_1.at[s]).wait()
@@ -616,7 +648,7 @@
     lax.fori_loop(1, 16, send_ring, 0)
 
     await_rims(me, grd, grad_sems)
-    stack_taps(grd, stack)
+    stack_taps(grd, stack, 0, 12)
 
     def inputs(at, carry):
         back = jnp.dot(wf[...], window(stack, at), preferred_element_type=F32)
@@ -627,7 +659,7 @@
             flat[strided(i), :] = grads[i] + slope * back[:, 128 * r : 128 * r + 128]
         return carry
 
-    lax.fori_loop(0, 8, inputs, 0)
+    lax.fori_loop(0, 4, inputs, 0)
 
     def wait_ring(t, carry):
         o = lax.rem(me.z + t, 16)
@@ -648,6 +680,8 @@
 
     lax.fori_loop(1, 32, send_all, 0)
 
+    lax.fori_loop(4, 8, inputs, 0)
+
     def narrow(c, carry):
         grad_out[c] = flat[pl.ds(pl.multiple_of(c * 64, 64), 64), :].astype(BF16)
         return carry
@@ -661,26 +695,24 @@
 
     lax.fori_loop(1, 32, wait_all, 0)
     for s in range(32):
-        whole[10 * s : 10 * s + 10, :] = dst[s]
-    for k in range(9):
-        t, half = k // 2, k % 2
-        cw_out[k] = whole[64 * t : 64 * t + 64, 64 * half : 64 * half + 64] / count
-    wh_out[...] = whole[256 : 256 + NB, 64:128] / count
-    cb_out[...] = whole[318:319, 64:128] / count
-    hb_out[...] = whole[319:320, 64 : 64 + NB] / count
-
+        sums_out[10 * s : 10 * s + 10, :] = dst[s]
     await_sent_rims(me, act, act_sems)
     await_sent_rims(me, grd, grad_sems)
 
     def sent_mirror(k, carry):
         for h in range(2):
-            @pl.when(jnp.logical_not(me.is_me(me.mirror_first(k))))
-            def _():
-                pltpu.make_async_copy(packed.at[h, piece(k)], tmp.at[0, h], a_send.at[k, h]).wait()
-
-            @pl.when(jnp.logical_not(me.is_me(me.mirror_second(k, h))))
-            def _():
-                pltpu.make_async_copy(tmp.at[k, h], placed.at[0, piece(0)], b_send.at[k, h]).wait()
+            for part in range(2):
+                @pl.when(jnp.logical_not(me.is_me(me.mirror_first(k))))
+                def _():
+                    pltpu.make_async_copy(
+                        piece(packed, h, k, part), tmp.at[part, 0, h], a_send.at[part, k, h]
+                    ).wait()
+
+                @pl.when(jnp.logical_not(me.is_me(me.mirror_second(k, h))))
+                def _():
+                    pltpu.make_async_copy(
+                        tmp.at[part, k, h], piece(placed, 0, 0, part), b_send.at[part, k, h]
+                    ).wait()
         return carry
 
     lax.fori_loop(0, 16, sent_mirror, 0)
@@ -699,6 +731,17 @@
         return carry
 
     lax.fori_loop(1, 16, sent_ring, 0)
+
+
+def finish(grad, sums, mask, grad_out, cw_out, cb_out, wh_out, hb_out):
+    count = jnp.sum(mask[...].astype(F32), keepdims=True)
+    for k in range(9):
+        t, half = k // 2, k % 2
+        cw_out[k] = sums[64 * t : 64 * t + 64, 64 * half : 64 * half + 64] / count
+    wh_out[...] = sums[256 : 256 + NB, 64:128] / count
+    cb_out[...] = sums[318:319, 64:128] / count
+    hb_out[...] = sums[319:320, 64 : 64 + NB] / count
+    grad_out[...] = grad[...]
 
 
 def per_device(
@@ -726,6 +769,7 @@
         pltpu.VMEM((12,) + cells, BF16),
         pltpu.VMEM((2, 2) + cells, BF16),
         pltpu.VMEM((64,) + cells, F32),
+        pltpu.VMEM((64,) + cells, BF16),
         pltpu.VMEM((64, 576), BF16),
         pltpu.VMEM((64, 576), BF16),
         pltpu.VMEM((64, 64), BF16),
@@ -733,7 +777,7 @@
         pltpu.VMEM(cells, F32),
         pltpu.VMEM(cells, F32),
         pltpu.VMEM((2, 32) + cells, BF16),
-        pltpu.VMEM((16, 2, 2) + cells, BF16),
+        pltpu.VMEM((2, 16, 2, 2, 32, 128), BF16),
         pltpu.VMEM((2, 32) + cells, BF16),
         pltpu.VMEM((2,) + cells, F32),
         pltpu.VMEM((64, 640), F32),
@@ -743,23 +787,21 @@
         pltpu.VMEM((320, 128), F32),
         pltpu.VMEM((16, 10, 128), F32),
         pltpu.VMEM((32, 10, 128), F32),
-        dma((16, 2)), dma((16, 2)), dma((16, 2)), dma((2, 16)),
+        dma((2, 16, 2)), dma((2, 16, 2)), dma((2, 16, 2)), dma((2, 2, 16)),
         dma((32,)), dma((32,)), dma((16,)), dma((16,)), dma((32,)), dma((32,)),
     ] + 2 * [
         dma((2,)), dma((2,)), dma((2, 4)), dma((2, 4)), dma((2, 4)), dma((2,)),
         dma((2,)), dma((2, 2)), dma((2, 2)),
     ]
-    grad_input, conv_w, conv_b, head_w, head_b = pl.pallas_call(
+    present = residue_mask.reshape(16, 128)
+    grad, sums = pl.pallas_call(
         kernel,
         out_shape=(
             jax.ShapeDtypeStruct(features.shape, BF16),
-            jax.ShapeDtypeStruct((9, 64, 64), F32),
-            jax.ShapeDtypeStruct((1, 64), F32),
-            jax.ShapeDtypeStruct((NB, 64), F32),
-            jax.ShapeDtypeStruct((1, NB), F32),
+            jax.ShapeDtypeStruct((320, 128), F32),
         ),
         in_specs=[vmem] * 8,
-        out_specs=(vmem,) * 5,
+        out_specs=(vmem,) * 2,
         scratch_shapes=scratch,
         compiler_params=pltpu.CompilerParams(collective_id=1, has_side_effects=True),
         name="pair_head",
@@ -771,8 +813,21 @@
         head_bias.reshape(1, NB),
         dist_label,
         omega_label,
-        residue_mask.reshape(16, 128),
-    )
+        present,
+    )
+    grad_input, conv_w, conv_b, head_w, head_b = pl.pallas_call(
+        finish,
+        out_shape=(
+            jax.ShapeDtypeStruct(features.shape, BF16),
+            jax.ShapeDtypeStruct((9, 64, 64), F32),
+            jax.ShapeDtypeStruct((1, 64), F32),
+            jax.ShapeDtypeStruct((NB, 64), F32),
+            jax.ShapeDtypeStruct((1, NB), F32),
+        ),
+        in_specs=[vmem] * 3,
+        out_specs=(vmem,) * 5,
+        name="scale",
+    )(grad, sums, present)
     return (
         grad_input,
         conv_w.reshape(3, 3, 64, 64),

time: 149 us -> 141 us (0.946)
  local copies, waits for them, and re-layouts: 4.67 us -> 0 us
  Pallas kernels: 143 us -> 140 us
    pallas_call x1, Pallas kernels: 143 us -> 137 us  [per_device(): pl.pallas_call(kernel, out_shape=(jax.ShapeDtypeStruct(features.shape, BF...]
    unnamed x13 -> x0, local copies, waits for them, and re-layouts: 4.67 us -> none
    pallas_call x0 -> x1, Pallas kernels: none -> 2.6 us  [per_device(): pl.pallas_call(finish, out_shape=(jax.ShapeDtypeStruct(features.shape, BF...]
where the time goes in v4:
time: 141 us; the launch traced here: 140 us
  Pallas kernels  140 us (99%)
    pallas_call x1, Pallas kernels, per_device(): pl.pallas_call(kernel, out_shape=(jax.ShapeDtypeStruct(features.shape, BF...  137 us

profile of v4, /device:TPU:1, one launch (start us, length us, event | category | flops | bytes accessed | tf_op | source)
XLA Modules:
  0.0 140.5 jit_solution(8786109425780994180)
XLA Ops:
  0.6 137.2 %pair_head.1 = (bf16[64,64,128]{2,1,0:T(8,128)(2,1)}, f32[320,128]{1,0:T(8,128)}) custom-call(bf16[64,64,128]{2,1,0:T(8,128)(2,1)} %feat.1, bf16[9,64,64]{2,1,0:T(8,128)(2,1)} %bitcast.7, f32[1,64]{1,0:T(1,128)} %bitcast.10, bf16[62,64]{1,0:T(8,128)(2,1)} %wh.1, f32[1,62]{1,0:T(1,128)} %bitcast.11, s32[64,128]{1,0:T(8,128)} %dist.1, s32[64,128]{1,0:T(8,128)} %omega.1, ...), custom_call_target="tpu_custom_call" | custom-call | tf_op jit(solution)/shard_map/pair_head/pallas_call | solution.py:797
  137.9 2.6 %scale.1 = (bf16[64,64,128]{2,1,0:T(8,128)(2,1)}, f32[9,64,64]{2,1,0:T(8,128)}, f32[1,64]{1,0:T(1,128)}, f32[62,64]{1,0:T(8,128)}, f32[1,62]{1,0:T(1,128)}) custom-call(bf16[64,64,128]{2,1,0:T(8,128)(2,1)} %get-tuple-element.12.grad, f32[320,128]{1,0:T(8,128)} %get-tuple-element.13.sums, s32[16,128]{1,0:T(8,128)} %bitcast.9), custom_call_target="tpu_custom_call" | custom-call | tf_op jit(solution)/shard_map/scale/pallas_call | solution.py:818

commit v5 on v4

--- a/solution.py
+++ b/solution.py
@@ -33,17 +33,14 @@
         self.z = 4 * self.block + lax.rem(chip, 4)
         self.spot = 4 * self.y + self.x
 
-    def is_me(self, t):
-        return (t[0] == self.x) & (t[1] == self.y) & (t[2] == self.z) & (t[3] == self.core)
+    def mirrors_itself(self):
+        return self.spot == self.z
 
     def mirror_first(self, k):
         return (lax.rem(k, 4), k // 4, self.z, self.core)
 
     def mirror_second(self, s, half):
         return (lax.rem(self.z, 4), self.z // 4, s, half)
-
-    def mirror_giver(self, k, core):
-        return (lax.rem(k, 4), k // 4, self.spot, core)
 
     def plane(self, s):
         return (lax.rem(s // 2, 4), s // 8, self.z, lax.rem(s, 2))
@@ -116,30 +113,25 @@
 
     lax.fori_loop(0, 4, far_partners, 0)
 
-    def mirror_partners(s, carry):
-        for t in (me.mirror_first(s), me.mirror_giver(s, 0), me.mirror_giver(s, 1)):
-            @pl.when(jnp.logical_not(me.is_me(t)))
-            def _():
-                signal(barrier, device(*t))
-        return carry
-
-    lax.fori_loop(0, 16, mirror_partners, 0)
-
-    def plane_partners(t, carry):
-        signal(barrier, device(*me.plane(lax.rem(me.plane_slot() + t, 32))))
-        return carry
-
-    lax.fori_loop(1, 32, plane_partners, 0)
-
-    def ring_partners(t, carry):
-        signal(barrier, device(*me.ring(lax.rem(me.z + t, 16))))
-        return carry
-
-    lax.fori_loop(1, 16, ring_partners, 0)
+    spot_row, spot_col = (me.z // 4) * 4, 2 * lax.rem(me.z, 4)
+    giver_row, giver_col = 4 * me.y, 2 * me.x
+    for k in range(16):
+        for core in range(2):
+            @pl.when(jnp.logical_not((me.spot == k) & (me.core == core)))
+            def _():
+                signal(barrier, (spot_row + k % 4, spot_col + 8 * (k // 4) + core))
+
+            @pl.when(jnp.logical_not(me.mirrors_itself() & (me.spot == k) & (me.core == core)))
+            def _():
+                signal(barrier, (giver_row + k % 4, giver_col + 8 * (k // 4) + core))
+
+        @pl.when(me.z != k)
+        def _():
+            signal(barrier, (me.x + 4 * (k // 4), 8 * me.y + 2 * (k % 4) + me.core))
 
 
 def await_greetings(me, barrier):
-    total = 46 + 47 - jnp.where(me.spot == me.z, 1, 0)
+    total = 31 + 15 + 32 - jnp.where(me.mirrors_itself(), 1, 0)
     for k in range(2):
         for known in (col_open(me, k), near(me, k), far_open(me, k)):
             total = total + jnp.where(known, 1, 0)
@@ -428,48 +420,54 @@
             logit[strided(at * 8 + r), :] = out[:, 128 * r : 128 * r + 128]
         return carry
 
-    def pack(part):
-        low = lax.broadcasted_iota(jnp.int32, (32, 128), 1) < 64
-        at = 32 * part
+    def pack(half):
+        group = lax.broadcasted_iota(jnp.int32, (32, 128), 1) // 32
+        at = 32 * half
 
         def step(m, carry):
-            one = logit[pl.ds(pl.multiple_of(m * 64 + at, 32), 32), :]
-            two = logit[pl.ds(pl.multiple_of(m * 64 + 2048 + at, 32), 32), :]
-            packed[0, m, at : at + 32] = jnp.where(low, one, turn(two, 64)).astype(BF16)
-            packed[1, m, at : at + 32] = jnp.where(low, turn(one, 64), two).astype(BF16)
+            four = [
+                logit[pl.ds(pl.multiple_of(m * 64 + 1024 * q + at, 32), 32), :] for q in range(4)
+            ]
+            for g in range(4):
+                out = turn(four[0], -32 * g)
+                for q in range(1, 4):
+                    out = jnp.where(group == q, turn(four[q], 32 * (q - g)), out)
+                packed[g // 2, g % 2, m, at : at + 32] = out.astype(BF16)
             return carry
 
-        lax.fori_loop(0, 32, step, 0)
+        lax.fori_loop(0, 16, step, 0)
 
     def piece(ref, h, k, part):
-        return ref.at[h, pl.ds(k * 2, 2), pl.ds(32 * part, 32)]
+        return ref.at[h, lax.rem(part, 2), k, pl.ds(pl.multiple_of(32 * (part // 2), 32), 32)]
 
     apart = lax.rem(me.spot - me.z + 16, 16)
     apart = lax.rem(jnp.minimum(apart, 16 - apart), 8)
 
-    def mirror_a(part):
-        def step(t, carry):
-            k = lax.rem(apart - t // 2 + 8, 8) + 8 * lax.rem(t, 2)
-            to = me.mirror_first(k)
-            for h in range(2):
-                @pl.when(me.is_me(to))
-                def _():
-                    pltpu.make_async_copy(
-                        piece(packed, h, k, part), tmp.at[part, me.spot, h],
-                        a_recv.at[part, me.spot, h],
-                    ).start()
-
-                @pl.when(jnp.logical_not(me.is_me(to)))
-                def _():
-                    remote(
-                        piece(packed, h, k, part), tmp.at[part, me.spot, h],
-                        a_send.at[part, k, h], a_recv.at[part, me.spot, h], device(*to),
-                    ).start()
-            return carry
-
-        lax.fori_loop(0, 16, step, 0)
-
-    def mirror_b(part, t):
+    def mirror_a(at, carry):
+        part, t = at // 16, lax.rem(at, 16)
+        k = lax.rem(apart - t // 2 + 8, 8) + 8 * lax.rem(t, 2)
+        to = device(*me.mirror_first(k))
+        for h in range(2):
+            @pl.when(k == me.spot)
+            def _():
+                pltpu.make_async_copy(
+                    piece(packed, h, k, part), tmp.at[part, me.spot, h],
+                    a_recv.at[part, me.spot, h],
+                ).start()
+
+            @pl.when(k != me.spot)
+            def _():
+                remote(
+                    piece(packed, h, k, part), tmp.at[part, me.spot, h],
+                    a_send.at[part, k, h], a_recv.at[part, me.spot, h], to,
+                ).start()
+        return carry
+
+    def at_home(s, h):
+        return me.mirrors_itself() & (s == me.z) & (me.core == h)
+
+    def mirror_b(at, carry):
+        part, t = at // 16, lax.rem(at, 16)
         p = lax.rem(me.spot + t // 2, 8)
         back = jnp.where(p == 0, 8, 16 - p)
         s = lax.rem(me.z + jnp.where(lax.rem(t, 2) == 0, p, back), 16)
@@ -477,74 +475,67 @@
             pltpu.make_async_copy(
                 piece(packed, h, 0, part), tmp.at[part, s, h], a_recv.at[part, s, h]
             ).wait()
-            to = me.mirror_second(s, h)
-
-            @pl.when(me.is_me(to))
+
+            @pl.when(at_home(s, h))
             def _():
                 pltpu.make_async_copy(
                     tmp.at[part, s, h], piece(placed, me.core, me.spot, part),
                     b_recv.at[part, me.core, me.spot],
                 ).start()
 
-            @pl.when(jnp.logical_not(me.is_me(to)))
+            @pl.when(jnp.logical_not(at_home(s, h)))
             def _():
                 remote(
                     tmp.at[part, s, h], piece(placed, me.core, me.spot, part),
-                    b_send.at[part, s, h], b_recv.at[part, me.core, me.spot], device(*to),
+                    b_send.at[part, s, h], b_recv.at[part, me.core, me.spot],
+                    device(*me.mirror_second(s, h)),
                 ).start()
+        return carry
 
     stack_taps(act, stack, 0, 8)
     lax.fori_loop(0, 4, forward, 0)
     pack(0)
-    mirror_a(0)
+    lax.fori_loop(0, 32, mirror_a, 0)
     stack_taps(act, stack, 8, 12)
 
     def forward_and_pass(at, carry):
         forward(at, carry)
-
-        def pass_on(u, inner):
-            mirror_b(0, (at - 4) * 4 + u)
-            return inner
-
-        lax.fori_loop(0, 4, pass_on, 0)
-        return carry
+        return lax.fori_loop((at - 4) * 8, (at - 3) * 8, mirror_b, carry)
 
     lax.fori_loop(4, 8, forward_and_pass, 0)
     pack(1)
-    mirror_a(1)
-
-    def pass_rest(t, carry):
-        mirror_b(1, t)
-        return carry
-
-    lax.fori_loop(0, 16, pass_rest, 0)
+    lax.fori_loop(32, 64, mirror_a, 0)
+    lax.fori_loop(32, 64, mirror_b, 0)
 
     mine_first = mask[pl.ds(me.col // 2, 1), :].astype(F32)
     mine_first = jnp.broadcast_to(mine_first, (128, 128)).T
     first = jnp.where(me.core == 0, mine_first[0:64], mine_first[64:128])
     pair = first * mask[pl.ds(me.row, 1), :].astype(F32)
 
-    def arrive(k, carry):
-        for c in range(2):
-            for part in range(2):
-                pltpu.make_async_copy(
-                    tmp.at[part, 0, 0], piece(placed, c, k, part), b_recv.at[part, c, k]
-                ).wait()
-        for u in range(2):
-            m = k * 2 + u
-            other = jnp.concatenate([placed[0, m], placed[1, m]], axis=0).astype(F32).T
-            one = pl.ds(pl.multiple_of(m * 64, 64), 64)
-            two = pl.ds(pl.multiple_of(m * 64 + 2048, 64), 64)
-            flat[one, :] = 0.5 * (logit[one, :] + other[0:64])
-            flat[two, :] = 0.5 * (logit[two, :] + other[64:128])
-        return carry
-
-    lax.fori_loop(0, 16, arrive, 0)
-    sums[0] = pair
+    sums[...] = jnp.zeros((3, 64, 128), F32)
+    sums[2] = pair
+    rows[...] = jnp.zeros((64, 640), F32)
+
+    def arrive(half):
+        def step(k, carry):
+            for c in range(2):
+                for here in range(2):
+                    part = 2 * here + half
+                    pltpu.make_async_copy(
+                        tmp.at[part, 0, 0], piece(placed, c, k, part), b_recv.at[part, c, k]
+                    ).wait()
+            other = jnp.concatenate([placed[0, half, k], placed[1, half, k]], axis=0)
+            other = other.astype(F32).T
+            for q in range(4):
+                at = pl.ds(pl.multiple_of(k * 64 + 1024 * q + 32 * half, 32), 32)
+                flat[at, :] = 0.5 * (logit[at, :] + other[32 * q : 32 * q + 32])
+            return carry
+
+        lax.fori_loop(0, 16, step, 0)
 
     def softmaxes(at, carry):
         eight = pl.ds(pl.multiple_of(at * 8, 8), 8)
-        weight = sums[0, eight, :]
+        weight = sums[2, eight, :]
         for start, stop, label in ((0, DB, dist), (DB, NB, omega)):
             chosen = label[eight, :]
             top = flat[block(start, at), :]
@@ -563,10 +554,6 @@
             flat[block(n, at), :] = jnp.zeros((8, 128), F32)
         return carry
 
-    lax.fori_loop(0, 8, softmaxes, 0)
-
-    rows[...] = jnp.zeros((64, 640), F32)
-    sums[...] = jnp.zeros((2, 64, 128), F32)
 
     def backward(at, carry):
         per_row = [flat[strided(at * 8 + r), :] for r in range(8)]
@@ -592,8 +579,6 @@
         gather_edges(rounded, gleft, gright, at)
         return carry
 
-    lax.fori_loop(0, 8, backward, 0)
-    send_rims(me, grd, grad_sems)
 
     def weights(at, carry):
         over_pairs = (((1,), (1,)), ((), ()))
@@ -606,7 +591,15 @@
         )
         return carry
 
-    lax.fori_loop(0, 8, weights, 0)
+    arrive(0)
+    lax.fori_loop(0, 4, softmaxes, 0)
+    lax.fori_loop(0, 4, backward, 0)
+    lax.fori_loop(0, 4, weights, 0)
+    arrive(1)
+    lax.fori_loop(4, 8, softmaxes, 0)
+    lax.fori_loop(4, 8, backward, 0)
+    send_rims(me, grd, grad_sems)
+    lax.fori_loop(4, 8, weights, 0)
     relay_rims(me, grd, grad_sems)
 
     rows[62:63, 576:640] = jnp.sum(sums[1].T, axis=0, keepdims=True)
@@ -628,6 +621,26 @@
     lax.fori_loop(1, 32, send_parts, 0)
     parts[slot] = src[slot]
 
+    await_sent_rims(me, act, act_sems)
+
+    def sent_mirror(at, carry):
+        part, k = at // 16, lax.rem(at, 16)
+        for h in range(2):
+            @pl.when(k != me.spot)
+            def _():
+                pltpu.make_async_copy(
+                    piece(packed, h, k, part), tmp.at[part, 0, h], a_send.at[part, k, h]
+                ).wait()
+
+            @pl.when(jnp.logical_not(at_home(k, h)))
+            def _():
+                pltpu.make_async_copy(
+                    tmp.at[part, k, h], piece(placed, 0, 0, part), b_send.at[part, k, h]
+                ).wait()
+        return carry
+
+    lax.fori_loop(0, 64, sent_mirror, 0)
+
     def wait_parts(t, carry):
         s = lax.rem(slot + t, 32)
         pltpu.make_async_copy(src.at[0], parts.at[s], recv_1.at[s]).wait()
@@ -687,6 +700,22 @@
         return carry
 
     lax.fori_loop(0, 64, narrow, 0)
+    await_sent_rims(me, grd, grad_sems)
+
+    def sent_sums(t, carry):
+        s = lax.rem(slot + t, 32)
+        pltpu.make_async_copy(mine.at[0], dst.at[s], send_1.at[s]).wait()
+        pltpu.make_async_copy(mine.at[0], dst.at[s], send_3.at[s]).wait()
+        return carry
+
+    lax.fori_loop(1, 32, sent_sums, 0)
+
+    def sent_ring(t, carry):
+        o = lax.rem(me.z + t, 16)
+        pltpu.make_async_copy(mine.at[0], ring.at[o], send_2.at[o]).wait()
+        return carry
+
+    lax.fori_loop(1, 16, sent_ring, 0)
 
     def wait_all(t, carry):
         s = lax.rem(slot + t, 32)
@@ -696,41 +725,6 @@
     lax.fori_loop(1, 32, wait_all, 0)
     for s in range(32):
         sums_out[10 * s : 10 * s + 10, :] = dst[s]
-    await_sent_rims(me, act, act_sems)
-    await_sent_rims(me, grd, grad_sems)
-
-    def sent_mirror(k, carry):
-        for h in range(2):
-            for part in range(2):
-                @pl.when(jnp.logical_not(me.is_me(me.mirror_first(k))))
-                def _():
-                    pltpu.make_async_copy(
-                        piece(packed, h, k, part), tmp.at[part, 0, h], a_send.at[part, k, h]
-                    ).wait()
-
-                @pl.when(jnp.logical_not(me.is_me(me.mirror_second(k, h))))
-                def _():
-                    pltpu.make_async_copy(
-                        tmp.at[part, k, h], piece(placed, 0, 0, part), b_send.at[part, k, h]
-                    ).wait()
-        return carry
-
-    lax.fori_loop(0, 16, sent_mirror, 0)
-
-    def sent_plane(t, carry):
-        s = lax.rem(slot + t, 32)
-        pltpu.make_async_copy(mine.at[0], dst.at[s], send_1.at[s]).wait()
-        pltpu.make_async_copy(mine.at[0], dst.at[s], send_3.at[s]).wait()
-        return carry
-
-    lax.fori_loop(1, 32, sent_plane, 0)
-
-    def sent_ring(t, carry):
-        o = lax.rem(me.z + t, 16)
-        pltpu.make_async_copy(mine.at[0], ring.at[o], send_2.at[o]).wait()
-        return carry
-
-    lax.fori_loop(1, 16, sent_ring, 0)
 
 
 def finish(grad, sums, mask, grad_out, cw_out, cb_out, wh_out, hb_out):
@@ -776,10 +770,10 @@
         pltpu.VMEM((64, 64), BF16),
         pltpu.VMEM(cells, F32),
         pltpu.VMEM(cells, F32),
-        pltpu.VMEM((2, 32) + cells, BF16),
-        pltpu.VMEM((2, 16, 2, 2, 32, 128), BF16),
-        pltpu.VMEM((2, 32) + cells, BF16),
-        pltpu.VMEM((2,) + cells, F32),
+        pltpu.VMEM((2, 2, 16) + cells, BF16),
+        pltpu.VMEM((4, 16, 2, 32, 128), BF16),
+        pltpu.VMEM((2, 2, 16) + cells, BF16),
+        pltpu.VMEM((3,) + cells, F32),
         pltpu.VMEM((64, 640), F32),
         pltpu.VMEM((32, 10, 128), F32),
         pltpu.VMEM((32, 10, 128), F32),
@@ -787,7 +781,7 @@
         pltpu.VMEM((320, 128), F32),
         pltpu.VMEM((16, 10, 128), F32),
         pltpu.VMEM((32, 10, 128), F32),
-        dma((2, 16, 2)), dma((2, 16, 2)), dma((2, 16, 2)), dma((2, 2, 16)),
+        dma((4, 16, 2)), dma((4, 16, 2)), dma((4, 16, 2)), dma((4, 2, 16)),
         dma((32,)), dma((32,)), dma((16,)), dma((16,)), dma((32,)), dma((32,)),
     ] + 2 * [
         dma((2,)), dma((2,)), dma((2, 4)), dma((2, 4)), dma((2, 4)), dma((2,)),

time: 141 us -> 136 us (0.965)
  Pallas kernels: 140 us -> 135 us
    pallas_call x1, Pallas kernels: 137 us -> 132 us  [per_device(): pl.pallas_call(kernel, out_shape=(jax.ShapeDtypeStruct(features.shape, BF...]
where the time goes in v5:
time: 136 us
  Pallas kernels  135 us (99%)
    pallas_call x1, Pallas kernels, per_device(): pl.pallas_call(kernel, out_shape=(jax.ShapeDtypeStruct(features.shape, BF...  132 us

profile of v5, /device:TPU:1, one launch (start us, length us, event | category | flops | bytes accessed | tf_op | source)
XLA Modules:
  0.0 135.6 jit_solution(5524172308440868926)
XLA Ops:
  0.6 132.4 %pair_head.1 = (bf16[64,64,128]{2,1,0:T(8,128)(2,1)}, f32[320,128]{1,0:T(8,128)}) custom-call(bf16[64,64,128]{2,1,0:T(8,128)(2,1)} %feat.1, bf16[9,64,64]{2,1,0:T(8,128)(2,1)} %bitcast.7, f32[1,64]{1,0:T(1,128)} %bitcast.10, bf16[62,64]{1,0:T(8,128)(2,1)} %wh.1, f32[1,62]{1,0:T(1,128)} %bitcast.11, s32[64,128]{1,0:T(8,128)} %dist.1, s32[64,128]{1,0:T(8,128)} %omega.1, ...), custom_call_target="tpu_custom_call" | custom-call | tf_op jit(solution)/shard_map/pair_head/pallas_call | solution.py:791
  133.0 2.6 %scale.1 = (bf16[64,64,128]{2,1,0:T(8,128)(2,1)}, f32[9,64,64]{2,1,0:T(8,128)}, f32[1,64]{1,0:T(1,128)}, f32[62,64]{1,0:T(8,128)}, f32[1,62]{1,0:T(1,128)}) custom-call(bf16[64,64,128]{2,1,0:T(8,128)(2,1)} %get-tuple-element.12.grad, f32[320,128]{1,0:T(8,128)} %get-tuple-element.13.sums, s32[16,128]{1,0:T(8,128)} %bitcast.9), custom_call_target="tpu_custom_call" | custom-call | tf_op jit(solution)/shard_map/scale/pallas_call | solution.py:812

commit v6 on v5

--- a/solution.py
+++ b/solution.py
@@ -356,11 +356,12 @@
 
 def kernel(
     feat, cw, cb, wh, hb, dist, omega, mask,
-    grad_out, sums_out,
+    grad_hbm, sums_out,
     flat, logit, held, own, left, right, from_left, from_right, via, stack, mixed,
     gown, gleft, gright, gfrom_left, gfrom_right, gvia, grads, glogit,
     wc, wf, whp, wht, bias_c, bias_h,
     packed, tmp, placed, sums, rows, src, parts, mine, whole, ring, dst,
+    narrowed, leave_sem,
     a_send, a_recv, b_send, b_recv,
     send_1, recv_1, send_2, recv_2, send_3, recv_3,
     *rim_sems,
@@ -432,13 +433,17 @@
                 out = turn(four[0], -32 * g)
                 for q in range(1, 4):
                     out = jnp.where(group == q, turn(four[q], 32 * (q - g)), out)
-                packed[g // 2, g % 2, m, at : at + 32] = out.astype(BF16)
+                packed[g % 2, m, g // 2, at : at + 32] = out.astype(BF16)
             return carry
 
         lax.fori_loop(0, 16, step, 0)
 
     def piece(ref, h, k, part):
         return ref.at[h, lax.rem(part, 2), k, pl.ds(pl.multiple_of(32 * (part // 2), 32), 32)]
+
+    def both(k, part):
+        at = pl.ds(pl.multiple_of(32 * (part // 2), 32), 32)
+        return packed.at[lax.rem(part, 2), k, :, at]
 
     apart = lax.rem(me.spot - me.z + 16, 16)
     apart = lax.rem(jnp.minimum(apart, 16 - apart), 8)
@@ -447,20 +452,19 @@
         part, t = at // 16, lax.rem(at, 16)
         k = lax.rem(apart - t // 2 + 8, 8) + 8 * lax.rem(t, 2)
         to = device(*me.mirror_first(k))
-        for h in range(2):
-            @pl.when(k == me.spot)
-            def _():
-                pltpu.make_async_copy(
-                    piece(packed, h, k, part), tmp.at[part, me.spot, h],
-                    a_recv.at[part, me.spot, h],
-                ).start()
-
-            @pl.when(k != me.spot)
-            def _():
-                remote(
-                    piece(packed, h, k, part), tmp.at[part, me.spot, h],
-                    a_send.at[part, k, h], a_recv.at[part, me.spot, h], to,
-                ).start()
+
+        @pl.when(k == me.spot)
+        def _():
+            pltpu.make_async_copy(
+                both(k, part), tmp.at[part, me.spot], a_recv.at[part, me.spot]
+            ).start()
+
+        @pl.when(k != me.spot)
+        def _():
+            remote(
+                both(k, part), tmp.at[part, me.spot],
+                a_send.at[part, k], a_recv.at[part, me.spot], to,
+            ).start()
         return carry
 
     def at_home(s, h):
@@ -471,11 +475,8 @@
         p = lax.rem(me.spot + t // 2, 8)
         back = jnp.where(p == 0, 8, 16 - p)
         s = lax.rem(me.z + jnp.where(lax.rem(t, 2) == 0, p, back), 16)
+        pltpu.make_async_copy(both(0, part), tmp.at[part, s], a_recv.at[part, s]).wait()
         for h in range(2):
-            pltpu.make_async_copy(
-                piece(packed, h, 0, part), tmp.at[part, s, h], a_recv.at[part, s, h]
-            ).wait()
-
             @pl.when(at_home(s, h))
             def _():
                 pltpu.make_async_copy(
@@ -625,13 +626,12 @@
 
     def sent_mirror(at, carry):
         part, k = at // 16, lax.rem(at, 16)
+
+        @pl.when(k != me.spot)
+        def _():
+            pltpu.make_async_copy(both(k, part), tmp.at[part, 0], a_send.at[part, k]).wait()
+
         for h in range(2):
-            @pl.when(k != me.spot)
-            def _():
-                pltpu.make_async_copy(
-                    piece(packed, h, k, part), tmp.at[part, 0, h], a_send.at[part, k, h]
-                ).wait()
-
             @pl.when(jnp.logical_not(at_home(k, h)))
             def _():
                 pltpu.make_async_copy(
@@ -696,10 +696,12 @@
     lax.fori_loop(4, 8, inputs, 0)
 
     def narrow(c, carry):
-        grad_out[c] = flat[pl.ds(pl.multiple_of(c * 64, 64), 64), :].astype(BF16)
+        narrowed[c] = flat[pl.ds(pl.multiple_of(c * 64, 64), 64), :].astype(BF16)
         return carry
 
     lax.fori_loop(0, 64, narrow, 0)
+    leave = pltpu.make_async_copy(narrowed, grad_hbm, leave_sem.at[0])
+    leave.start()
     await_sent_rims(me, grd, grad_sems)
 
     def sent_sums(t, carry):
@@ -725,17 +727,21 @@
     lax.fori_loop(1, 32, wait_all, 0)
     for s in range(32):
         sums_out[10 * s : 10 * s + 10, :] = dst[s]
+    leave.wait()
 
 
 def finish(grad, sums, mask, grad_out, cw_out, cb_out, wh_out, hb_out):
-    count = jnp.sum(mask[...].astype(F32), keepdims=True)
-    for k in range(9):
-        t, half = k // 2, k % 2
-        cw_out[k] = sums[64 * t : 64 * t + 64, 64 * half : 64 * half + 64] / count
-    wh_out[...] = sums[256 : 256 + NB, 64:128] / count
-    cb_out[...] = sums[318:319, 64:128] / count
-    hb_out[...] = sums[319:320, 64 : 64 + NB] / count
     grad_out[...] = grad[...]
+
+    @pl.when(pl.program_id(0) == 0)
+    def _():
+        count = jnp.sum(mask[...].astype(F32), keepdims=True)
+        for k in range(9):
+            t, half = k // 2, k % 2
+            cw_out[k] = sums[64 * t : 64 * t + 64, 64 * half : 64 * half + 64] / count
+        wh_out[...] = sums[256 : 256 + NB, 64:128] / count
+        cb_out[...] = sums[318:319, 64:128] / count
+        hb_out[...] = sums[319:320, 64 : 64 + NB] / count
 
 
 def per_device(
@@ -770,7 +776,7 @@
         pltpu.VMEM((64, 64), BF16),
         pltpu.VMEM(cells, F32),
         pltpu.VMEM(cells, F32),
-        pltpu.VMEM((2, 2, 16) + cells, BF16),
+        pltpu.VMEM((2, 16, 2) + cells, BF16),
         pltpu.VMEM((4, 16, 2, 32, 128), BF16),
         pltpu.VMEM((2, 2, 16) + cells, BF16),
         pltpu.VMEM((3,) + cells, F32),
@@ -781,7 +787,9 @@
         pltpu.VMEM((320, 128), F32),
         pltpu.VMEM((16, 10, 128), F32),
         pltpu.VMEM((32, 10, 128), F32),
-        dma((4, 16, 2)), dma((4, 16, 2)), dma((4, 16, 2)), dma((4, 2, 16)),
+        pltpu.VMEM((64,) + cells, BF16),
+        dma((1,)),
+        dma((4, 16)), dma((4, 16)), dma((4, 16, 2)), dma((4, 2, 16)),
         dma((32,)), dma((32,)), dma((16,)), dma((16,)), dma((32,)), dma((32,)),
     ] + 2 * [
         dma((2,)), dma((2,)), dma((2, 4)), dma((2, 4)), dma((2, 4)), dma((2,)),
@@ -795,7 +803,7 @@
             jax.ShapeDtypeStruct((320, 128), F32),
         ),
         in_specs=[vmem] * 8,
-        out_specs=(vmem,) * 2,
+        out_specs=(pl.BlockSpec(memory_space=pl.ANY), vmem),
         scratch_shapes=scratch,
         compiler_params=pltpu.CompilerParams(collective_id=1, has_side_effects=True),
         name="pair_head",
@@ -818,8 +826,19 @@
             jax.ShapeDtypeStruct((NB, 64), F32),
             jax.ShapeDtypeStruct((1, NB), F32),
         ),
-        in_specs=[vmem] * 3,
-        out_specs=(vmem,) * 5,
+        grid=(4,),
+        in_specs=[
+            pl.BlockSpec((16, 64, 128), lambda c: (c, 0, 0)),
+            pl.BlockSpec((320, 128), lambda c: (0, 0)),
+            pl.BlockSpec((16, 128), lambda c: (0, 0)),
+        ],
+        out_specs=(
+            pl.BlockSpec((16, 64, 128), lambda c: (c, 0, 0)),
+            pl.BlockSpec((9, 64, 64), lambda c: (0, 0, 0)),
+            pl.BlockSpec((1, 64), lambda c: (0, 0)),
+            pl.BlockSpec((NB, 64), lambda c: (0, 0)),
+            pl.BlockSpec((1, NB), lambda c: (0, 0)),
+        ),
         name="scale",
     )(grad, sums, present)
     return (

time: 136 us -> 135 us (level)
    pallas_call x1, Pallas kernels: 132 us -> 130 us  [per_device(): pl.pallas_call(kernel, out_shape=(jax.ShapeDtypeStruct(features.shape, BF...]
where the time goes in v6:
time: 135 us
  Pallas kernels  134 us (99%)
    pallas_call x1, Pallas kernels, per_device(): pl.pallas_call(kernel, out_shape=(jax.ShapeDtypeStruct(features.shape, BF...  130 us
    pallas_call x1, Pallas kernels, per_device(): pl.pallas_call(finish, out_shape=(jax.ShapeDtypeStruct(features.shape, BF...  3.79 us

profile of v6, /device:TPU:1, one launch (start us, length us, event | category | flops | bytes accessed | tf_op | source)
XLA Modules:
  0.0 134.8 jit_solution(7310410413918157959)
XLA Ops:
  0.6 130.3 %pair_head.1 = (bf16[64,64,128]{2,1,0:T(8,128)(2,1)}, f32[320,128]{1,0:T(8,128)}) custom-call(bf16[64,64,128]{2,1,0:T(8,128)(2,1)} %feat.1, bf16[9,64,64]{2,1,0:T(8,128)(2,1)} %bitcast.7, f32[1,64]{1,0:T(1,128)} %bitcast.10, bf16[62,64]{1,0:T(8,128)(2,1)} %wh.1, f32[1,62]{1,0:T(1,128)} %bitcast.11, s32[64,128]{1,0:T(8,128)} %dist.1, s32[64,128]{1,0:T(8,128)} %omega.1, ...), custom_call_target="tpu_custom_call" | custom-call | tf_op jit(solution)/shard_map/pair_head/pallas_call | solution.py:799
  131.0 3.8 %scale.1 = (bf16[64,64,128]{2,1,0:T(8,128)(2,1)}, f32[9,64,64]{2,1,0:T(8,128)}, f32[1,64]{1,0:T(1,128)}, f32[62,64]{1,0:T(8,128)}, f32[1,62]{1,0:T(1,128)}) custom-call(bf16[64,64,128]{2,1,0:T(8,128)(2,1)} %get-tuple-element.12.grad, f32[320,128]{1,0:T(8,128)} %get-tuple-element.13.sums, s32[16,128]{1,0:T(8,128)} %bitcast.9), custom_call_target="tpu_custom_call" | custom-call | tf_op jit(solution)/shard_map/scale/pallas_call | solution.py:820
